TPU v7x, 32 devices: a whole 2x2x4 slice. The times are simulated.
32 devices in a mesh: row: 8 (over z, y), col: 4 (over x, core).
Axes of the slice: x: 2, y: 2, z: 4, core: 2. Of those that a mesh axis runs over, the one named last changes fastest.
Arguments:
- object_tiles: float32 [2, 2, 3072, 1536], P(None, None, 'row', 'col'), may hold values from -4 to 4
- probe_field: float32 [2, 128, 128], replicated, may hold values from -4 to 4
- prop_phase: float32 [128, 128], replicated, may hold values from -3.140625 to 3.140625
- intensity: float32 [256, 128, 128], P(('row', 'col')), may hold values from 0 to 2
- positions: int32 [256, 2], P(('row', 'col')), may hold values from 0 to 383
- counts: int32 [8, 4], P('row'), may hold values from 1 to 8, as said below
Outputs:
- object_new: float32 [2, 2, 3072, 1536], P(None, None, 'row', 'col')
Inputs may be any that keep to these rules, and one draw needn't show every extreme that they name: `counts`: in each row of the tile grid, in every aligned group of four tile columns 4j to 4j + 3, exactly two entries equal 8, and they sit at columns 4j and 4j + 1, or 4j + 2 and 4j + 3, or 4j and 4j + 2, or 4j + 1 and 4j + 3; the other two lie between 1 and 4.
All inputs are finite; a program needn't handle non-finite values.
Results may differ from a plain program's by a relative error of at most 0.0003.
Values sent between devices are 32-bit elements; how exact they have to be, the bound alone decides.
A program may use at most 64 MiB of HBM per device.

v0:
```python
import functools

import jax
import jax.numpy as jnp
import numpy as np
from jax import lax
from jax.experimental import pallas as pl
from jax.experimental.pallas import tpu as pltpu
from jax.sharding import PartitionSpec as P

ITERS = 2
GROUP = 4
SUB = 8

step_size = 0.2


def dft_tables(size):
    index = np.arange(size)
    phase = (index[:, None] * index[None, :] % size) * (2.0 * np.pi / size)
    re = np.cos(phase) / np.sqrt(size)
    im = -np.sin(phase) / np.sqrt(size)
    rights, lefts = [], []
    for sign in (1.0, -1.0):
        right = np.block([[re, sign * im], [-sign * im, re]]).astype(np.float32)
        high = right.astype(jnp.bfloat16)
        low = (right - high.astype(np.float32)).astype(jnp.bfloat16)
        rights.append(np.concatenate([high, high, low], axis=0))
        lefts.append(np.concatenate([high.T, high.T, low.T], axis=1))
    return np.stack(rights), np.stack(lefts)


def split(x):
    high = x.astype(jnp.bfloat16)
    low = (x - high.astype(jnp.float32)).astype(jnp.bfloat16)
    return high, low


def by_right(waves, table):
    size = waves[0][0].shape[0]
    x = jnp.concatenate([jnp.concatenate(wave, axis=1) for wave in waves], axis=0)
    high, low = split(x)
    y = jnp.dot(
        jnp.concatenate([high, low, high], axis=1), table, preferred_element_type=jnp.float32
    )
    return [
        (y[i * size : (i + 1) * size, :size], y[i * size : (i + 1) * size, size:])
        for i in range(len(waves))
    ]


def by_left(waves, table):
    size = waves[0][0].shape[0]
    x = jnp.concatenate([jnp.concatenate(wave, axis=0) for wave in waves], axis=1)
    high, low = split(x)
    y = jnp.dot(
        table, jnp.concatenate([high, low, high], axis=0), preferred_element_type=jnp.float32
    )
    return [
        (y[:size, i * size : (i + 1) * size], y[size:, i * size : (i + 1) * size])
        for i in range(len(waves))
    ]


def mul(a, b):
    return (a[0] * b[0] - a[1] * b[1], a[0] * b[1] + a[1] * b[0])


def conj_mul(a, b):
    return (a[0] * b[0] + a[1] * b[1], a[0] * b[1] - a[1] * b[0])


def frames_kernel(
    counts_ref, pos_ref, main_hbm, right_hbm, below_hbm, corner_hbm, probe_ref, kern_ref,
    meas_ref, rtab_ref, ltab_ref, out_main, out_right, out_below, out_corner, ext, grad, sems,
):
    frame = probe_ref.shape[1]
    tile = main_hbm.shape[1]
    slots = meas_ref.shape[0]
    whole = tile + frame
    copies = [
        pltpu.make_async_copy(main_hbm, ext.at[:, pl.ds(0, tile), pl.ds(0, tile)], sems.at[0]),
        pltpu.make_async_copy(right_hbm, ext.at[:, pl.ds(0, tile), pl.ds(tile, frame)], sems.at[1]),
        pltpu.make_async_copy(below_hbm, ext.at[:, pl.ds(tile, frame), pl.ds(0, tile)], sems.at[2]),
        pltpu.make_async_copy(
            corner_hbm, ext.at[:, pl.ds(tile, frame), pl.ds(tile, frame)], sems.at[3]
        ),
    ]
    for copy in copies:
        copy.start()
    grad[...] = jnp.zeros_like(grad)
    for copy in copies:
        copy.wait()
    count = counts_ref[0]
    lane = lax.broadcasted_iota(jnp.int32, (frame + SUB, frame), 1)
    sub = lax.broadcasted_iota(jnp.int32, (frame // SUB + 1, SUB, frame), 1)
    edge = jnp.zeros((1, SUB, frame), jnp.float32)

    @pl.loop(0, (count + GROUP - 1) // GROUP)
    def _(group):
        places, firsts, seconds = [], [], []
        for i in range(GROUP):
            slot = group * GROUP + i
            here = jnp.minimum(slot, slots - 1)
            weight = (slot < count).astype(jnp.float32)
            top = pos_ref[2 * here]
            left = pos_ref[2 * here + 1]
            block = left // frame
            shift = left - block * frame
            near = pl.ds(pl.multiple_of(block * frame, frame), frame)
            far = pl.ds(pl.multiple_of(block * frame + frame, frame), frame)
            start = top // SUB * SUB
            drop = top - start
            rows = pl.ds(pl.multiple_of(start, SUB), frame + SUB)
            back = lax.rem(frame - shift, frame)
            lift = lax.rem(SUB - drop, SUB)
            planes = []
            for s in range(4):
                a = pltpu.roll(ext[s, rows, near], back, 1)
                b = pltpu.roll(ext[s, rows, far], back, 1)
                wide = jnp.where(lane < frame - shift, a, b).reshape(-1, SUB, frame)
                wide = pltpu.roll(wide, lift, 1)
                plane = jnp.where(sub[1:] < SUB - drop, wide[:-1], wide[1:])
                planes.append(plane.reshape(frame, frame))
            places.append((here, weight, rows, near, far, shift, drop))
            firsts.append((planes[0], planes[1]))
            seconds.append((planes[2], planes[3]))
        probe = (probe_ref[0], probe_ref[1])
        kern = (kern_ref[0], kern_ref[1])
        lit = [mul(probe, first) for first in firsts]
        freq = by_left(by_right(lit, rtab_ref[0]), ltab_ref[0])
        moved = [mul(kern, f) for f in freq]
        inner = by_right(by_left(moved, ltab_ref[1]), rtab_ref[1])
        leave = [mul(b, o) for b, o in zip(inner, seconds)]
        far_field = by_left(by_right(leave, rtab_ref[0]), ltab_ref[0])
        missed = []
        for place, (re, im) in zip(places, far_field):
            misfit = re * re + im * im - meas_ref[place[0]]
            missed.append((misfit * re, misfit * im))
        back_wave = by_right(by_left(missed, ltab_ref[1]), rtab_ref[1])
        grad_two = [conj_mul(b, g) for b, g in zip(inner, back_wave)]
        carry = [conj_mul(o, g) for o, g in zip(seconds, back_wave)]
        carried = by_left(by_right(carry, rtab_ref[0]), ltab_ref[0])
        unmoved = [conj_mul(kern, f) for f in carried]
        near_wave = by_right(by_left(unmoved, ltab_ref[1]), rtab_ref[1])
        grad_one = [conj_mul(probe, w) for w in near_wave]
        for place, one, two in zip(places, grad_one, grad_two):
            here, weight, rows, near, far, shift, drop = place
            for s, value in enumerate((one[0], one[1], two[0], two[1])):
                turned = pltpu.roll(value * weight, shift, 1).reshape(-1, SUB, frame)
                turned = pltpu.roll(turned, drop, 1)
                upper = jnp.concatenate([turned, edge], axis=0)
                lower = jnp.concatenate([edge, turned], axis=0)
                turned = jnp.where(sub >= drop, upper, lower).reshape(frame + SUB, frame)
                inside = lane >= shift
                grad[s, rows, near] += jnp.where(inside, turned, 0.0)
                grad[s, rows, far] += jnp.where(inside, 0.0, turned)

    outs = [
        pltpu.make_async_copy(grad.at[:, pl.ds(0, tile), pl.ds(0, tile)], out_main, sems.at[0]),
        pltpu.make_async_copy(grad.at[:, pl.ds(0, tile), pl.ds(tile, frame)], out_right, sems.at[1]),
        pltpu.make_async_copy(grad.at[:, pl.ds(tile, frame), pl.ds(0, tile)], out_below, sems.at[2]),
        pltpu.make_async_copy(
            grad.at[:, pl.ds(tile, frame), pl.ds(tile, frame)], out_corner, sems.at[3]
        ),
    ]
    for copy in outs:
        copy.start()
    for copy in outs:
        copy.wait()


def frame_grads(count, positions, main, right, below, corner, probe, kern, intensity, tables):
    frame = probe.shape[1]
    tile = main.shape[1]
    smem = pl.BlockSpec(memory_space=pltpu.SMEM)
    vmem = pl.BlockSpec(memory_space=pltpu.VMEM)
    anywhere = pl.BlockSpec(memory_space=pl.ANY)
    whole = tile + frame
    return pl.pallas_call(
        frames_kernel,
        out_shape=[
            jax.ShapeDtypeStruct((4, tile, tile), jnp.float32),
            jax.ShapeDtypeStruct((4, tile, frame), jnp.float32),
            jax.ShapeDtypeStruct((4, frame, tile), jnp.float32),
            jax.ShapeDtypeStruct((4, frame, frame), jnp.float32),
        ],
        in_specs=[smem, smem] + [anywhere] * 4 + [vmem] * 5,
        out_specs=[anywhere] * 4,
        scratch_shapes=[
            pltpu.VMEM((4, whole, whole), jnp.float32),
            pltpu.VMEM((4, whole, whole), jnp.float32),
            pltpu.SemaphoreType.DMA((4,)),
        ],
        compiler_params=pltpu.CompilerParams(vmem_limit_bytes=48 << 20),
    )(count, positions, main, right, below, corner, probe, kern, intensity, *tables)


def passed(x, by_row, by_col):
    rows, cols = lax.axis_size("row"), lax.axis_size("col")
    pairs = [
        (r * cols + c, (r + by_row) * cols + c + by_col)
        for r in range(rows)
        for c in range(cols)
        if 0 <= r + by_row < rows and 0 <= c + by_col < cols
    ]
    return lax.ppermute(x, ("row", "col"), pairs)


def local(object_tiles, probe_field, prop_phase, intensity, positions, counts):
    tile = object_tiles.shape[3]
    frame = probe_field.shape[1]
    tables = [jnp.asarray(t) for t in dft_tables(frame)]
    kern = jnp.stack([jnp.cos(prop_phase), jnp.sin(prop_phase)])
    count = lax.dynamic_slice(counts[0], (lax.axis_index("col"),), (1,))
    flat = positions.reshape(-1)
    current = object_tiles.reshape(4, tile, tile)
    for iteration in range(ITERS):
        right = passed(current[:, :, :frame], 0, -1)
        below = passed(current[:, :frame, :], -1, 0)
        corner = passed(current[:, :frame, :frame], -1, -1)
        g_main, g_right, g_below, g_corner = frame_grads(
            count, flat, current, right, below, corner, probe_field, kern, intensity, tables
        )
        g_right = passed(g_right, 0, 1)
        g_below = passed(g_below, 1, 0)
        g_corner = passed(g_corner, 1, 1)
        rest = tile - frame
        total = (
            g_main
            + jnp.pad(g_right, ((0, 0), (0, 0), (0, rest)))
            + jnp.pad(g_below, ((0, 0), (0, rest), (0, 0)))
            + jnp.pad(g_corner, ((0, 0), (0, rest), (0, rest)))
        )
        current = current - step_size * total
    return current.reshape(object_tiles.shape)


def solution(mesh):
    return jax.shard_map(
        local,
        mesh=mesh,
        in_specs=(
            P(None, None, "row", "col"),
            P(),
            P(),
            P(("row", "col"), None, None),
            P(("row", "col"), None),
            P("row", None),
        ),
        out_specs=P(None, None, "row", "col"),
        check_vma=False,
    )
```

profile of v0, /device:TPU:9, one launch (start us, length us, event | category | flops | bytes accessed | tf_op | source)
XLA Modules:
  0.0 158.7 jit_solution(17686790698373229300)
XLA Ops:
  0.0 2.2 %slice.24 = f32[4,384,128]{2,1,0:T(8,128)} slice(f32[4,384,384]{2,1,0:T(8,128)} %bitcast.8), slice={[0:4], [0:384], [0:128]} | slice | bytes 1572864 | tf_op jit(solution)/shard_map/slice | solution.py:219
  2.3 2.6 %collective-permute-start = (f32[4,384,128]{2,1,0:T(8,128)}, f32[4,384,128]{2,1,0:T(8,128)S(1)}, u32[]{:S(2)}, u32[]{:S(2)}) collective-permute-start(f32[4,384,128]{2,1,0:T(8,128)} %slice.24), channel_id=1, source_target_pairs={{1,0},{2,1},{3,2},{5,4},{6,5},{7,6},{9,8},{10,9},{11,10},{13,12},{... | collective-permute-start | bytes 2359304 | tf_op jit(solution)/shard_map/ppermute | solution.py:207
  4.8 2.1 %slice.25 = f32[4,128,384]{2,1,0:T(8,128)} slice(f32[4,384,384]{2,1,0:T(8,128)} %bitcast.9), slice={[0:4], [0:128], [0:384]} | slice | bytes 1572864 | tf_op jit(solution)/shard_map/slice | solution.py:220
  6.9 3.0 %collective-permute-start.1 = (f32[4,128,384]{2,1,0:T(8,128)}, f32[4,128,384]{2,1,0:T(8,128)}, u32[]{:S(2)}, u32[]{:S(2)}) collective-permute-start(f32[4,128,384]{2,1,0:T(8,128)} %slice.25), channel_id=1, source_target_pairs={{4,0},{5,1},{6,2},{7,3},{8,4},{9,5},{10,6},{11,7},{12,8},{13,9},{1... | collective-permute-start | bytes 2359304 | tf_op jit(solution)/shard_map/ppermute | solution.py:207
  10.9 1.9 %collective-permute-start.2 = (f32[4,128,128]{2,1,0:T(8,128)S(1)}, f32[4,128,128]{2,1,0:T(8,128)S(1)}, u32[]{:S(2)}, u32[]{:S(2)}) collective-permute-start(f32[4,128,128]{2,1,0:T(8,128)S(1)} %slice.26), channel_id=1, source_target_pairs={{5,0},{6,1},{7,2},{9,4},{10,5},{11,6},{13,8},{14,9},{15,10},{17,12... | collective-permute-start | bytes 786440 | tf_op jit(solution)/shard_map/ppermute | solution.py:207
  13.7 1.1 cosine_bitcast_fusion
  14.8 15.3 %collective-permute-done.2.corner_hbm = f32[4,128,128]{2,1,0:T(8,128)S(1)} collective-permute-done((f32[4,128,128]{2,1,0:T(8,128)S(1)}, f32[4,128,128]{2,1,0:T(8,128)S(1)}, u32[]{:S(2)}, u32[]{:S(2)}) %collective-permute-start.2) | collective-permute-done | bytes 262176 | tf_op jit(solution)/shard_map/ppermute | solution.py:207
  30.2 1.0 collective-permute-done.1.below_hbm
  31.2 9.9 %shard_map.82 = (f32[4,384,384]{2,1,0:T(8,128)}, f32[4,384,128]{2,1,0:T(8,128)S(1)}, f32[4,128,384]{2,1,0:T(8,128)S(1)}, f32[4,128,128]{2,1,0:T(8,128)S(1)}) custom-call(s32[1]{0:T(128)} %bitcast.1.counts_ref, s32[16]{0:T(128)S(1)} %reshape.11.pos_ref, f32[4,384,384]{2,1,0:T(8,128)} %bitcast.11, f32[4,384,128]{2,1,0:T(8,128)S(1)} %collective-permute-done.right_hbm, ...), custom_call_target="tpu_custom_call" | custom-call | tf_op jit(solution)/shard_map/pallas_call | solution.py:180
  41.1 10.6 %collective-permute-start.3 = (f32[4,384,128]{2,1,0:T(8,128)S(1)}, f32[4,384,128]{2,1,0:T(8,128)S(1)}, u32[]{:S(2)}, u32[]{:S(2)}) collective-permute-start(f32[4,384,128]{2,1,0:T(8,128)S(1)} %get-tuple-element.14), channel_id=1, source_target_pairs={{0,1},{1,2},{2,3},{4,5},{5,6},{6,7},{8,9},{9,10},{10,11},{12,13},{... | collective-permute-start | bytes 2359304 | tf_op jit(solution)/shard_map/ppermute | solution.py:207
  51.8 4.7 %collective-permute-start.4 = (f32[4,128,384]{2,1,0:T(8,128)S(1)}, f32[4,128,384]{2,1,0:T(8,128)S(1)}, u32[]{:S(2)}, u32[]{:S(2)}) collective-permute-start(f32[4,128,384]{2,1,0:T(8,128)S(1)} %get-tuple-element.15), channel_id=1, source_target_pairs={{0,4},{1,5},{2,6},{3,7},{4,8},{5,9},{6,10},{7,11},{8,12},{9,13},{1... | collective-permute-start | bytes 2359304 | tf_op jit(solution)/shard_map/ppermute | solution.py:207
  56.5 1.9 %collective-permute-start.5 = (f32[4,128,128]{2,1,0:T(8,128)S(1)}, f32[4,128,128]{2,1,0:T(8,128)S(1)}, u32[]{:S(2)}, u32[]{:S(2)}) collective-permute-start(f32[4,128,128]{2,1,0:T(8,128)S(1)} %get-tuple-element.16), channel_id=1, source_target_pairs={{0,5},{1,6},{2,7},{4,9},{5,10},{6,11},{8,13},{9,14},{10,15},{12,17... | collective-permute-start | bytes 786440 | tf_op jit(solution)/shard_map/ppermute | solution.py:207
  58.4 21.0 %collective-permute-done.5 = f32[4,128,128]{2,1,0:T(8,128)S(1)} collective-permute-done((f32[4,128,128]{2,1,0:T(8,128)S(1)}, f32[4,128,128]{2,1,0:T(8,128)S(1)}, u32[]{:S(2)}, u32[]{:S(2)}) %collective-permute-start.5) | collective-permute-done | bytes 262176 | tf_op jit(solution)/shard_map/ppermute | solution.py:207
  79.5 2.1 %multiply_subtract_fusion.1.main_hbm = f32[4,384,384]{2,1,0:T(8,128)S(1)} fusion(f32[4,128,128]{2,1,0:T(8,128)S(1)} %collective-permute-done.5, f32[4,128,384]{2,1,0:T(8,128)S(1)} %collective-permute-done.4, f32[4,384,384]{2,1,0:T(8,128)} %get-tuple-element.13, f32[4,384,128]{2,1,0:T(8,128)S(1)} %collective-permute-done.3, f32[2,2,384,384]{3,2,1,0:T(8,128)S(1)} %copy-done.6), kind=kLoop, calls=%fused_computation.1 | loop fusion | flops 2949120 | bytes 8912896 | tf_op jit(solution)/shard_map/sub | solution.py:235
  81.7 1.9 %collective-permute-start.6 = (f32[4,384,128]{2,1,0:T(8,128)S(1)}, f32[4,384,128]{2,1,0:T(8,128)S(1)}, u32[]{:S(2)}, u32[]{:S(2)}) collective-permute-start(f32[4,384,128]{2,1,0:T(8,128)S(1)} %slice.27), channel_id=1, source_target_pairs={{1,0},{2,1},{3,2},{5,4},{6,5},{7,6},{9,8},{10,9},{11,10},{13,12},{... | collective-permute-start | bytes 2359304 | tf_op jit(solution)/shard_map/ppermute | solution.py:207
  83.6 1.9 %collective-permute-start.7 = (f32[4,128,384]{2,1,0:T(8,128)S(1)}, f32[4,128,384]{2,1,0:T(8,128)S(1)}, u32[]{:S(2)}, u32[]{:S(2)}) collective-permute-start(f32[4,128,384]{2,1,0:T(8,128)S(1)} %slice.28), channel_id=1, source_target_pairs={{4,0},{5,1},{6,2},{7,3},{8,4},{9,5},{10,6},{11,7},{12,8},{13,9},{1... | collective-permute-start | bytes 2359304 | tf_op jit(solution)/shard_map/ppermute | solution.py:207
  85.6 1.9 %collective-permute-start.8 = (f32[4,128,128]{2,1,0:T(8,128)S(1)}, f32[4,128,128]{2,1,0:T(8,128)S(1)}, u32[]{:S(2)}, u32[]{:S(2)}) collective-permute-start(f32[4,128,128]{2,1,0:T(8,128)S(1)} %slice.29), channel_id=1, source_target_pairs={{5,0},{6,1},{7,2},{9,4},{10,5},{11,6},{13,8},{14,9},{15,10},{17,12... | collective-permute-start | bytes 786440 | tf_op jit(solution)/shard_map/ppermute | solution.py:207
  87.5 18.0 %collective-permute-done.8.corner_hbm = f32[4,128,128]{2,1,0:T(8,128)S(1)} collective-permute-done((f32[4,128,128]{2,1,0:T(8,128)S(1)}, f32[4,128,128]{2,1,0:T(8,128)S(1)}, u32[]{:S(2)}, u32[]{:S(2)}) %collective-permute-start.8) | collective-permute-done | bytes 262176 | tf_op jit(solution)/shard_map/ppermute | solution.py:207
  105.5 9.6 %shard_map.83 = (f32[4,384,384]{2,1,0:T(8,128)}, f32[4,384,128]{2,1,0:T(8,128)S(1)}, f32[4,128,384]{2,1,0:T(8,128)S(1)}, f32[4,128,128]{2,1,0:T(8,128)S(1)}) custom-call(s32[1]{0:T(128)} %bitcast.1.counts_ref, s32[16]{0:T(128)S(1)} %reshape.11.pos_ref, f32[4,384,384]{2,1,0:T(8,128)} %copy-done.5, f32[4,384,128]{2,1,0:T(8,128)S(1)} %collective-permute-done.6.right_hbm, ...), custom_call_target="tpu_custom_call" | custom-call | tf_op jit(solution)/shard_map/pallas_call | solution.py:180
  115.1 11.7 %collective-permute-start.9 = (f32[4,384,128]{2,1,0:T(8,128)S(1)}, f32[4,384,128]{2,1,0:T(8,128)S(1)}, u32[]{:S(2)}, u32[]{:S(2)}) collective-permute-start(f32[4,384,128]{2,1,0:T(8,128)S(1)} %get-tuple-element.18), channel_id=1, source_target_pairs={{0,1},{1,2},{2,3},{4,5},{5,6},{6,7},{8,9},{9,10},{10,11},{12,13},{... | collective-permute-start | bytes 2359304 | tf_op jit(solution)/shard_map/ppermute | solution.py:207
  126.9 5.3 %collective-permute-start.10 = (f32[4,128,384]{2,1,0:T(8,128)S(1)}, f32[4,128,384]{2,1,0:T(8,128)S(1)}, u32[]{:S(2)}, u32[]{:S(2)}) collective-permute-start(f32[4,128,384]{2,1,0:T(8,128)S(1)} %get-tuple-element.19), channel_id=1, source_target_pairs={{0,4},{1,5},{2,6},{3,7},{4,8},{5,9},{6,10},{7,11},{8,12},{9,13},{1... | collective-permute-start | bytes 2359304 | tf_op jit(solution)/shard_map/ppermute | solution.py:207
  132.2 1.9 %collective-permute-start.11 = (f32[4,128,128]{2,1,0:T(8,128)S(1)}, f32[4,128,128]{2,1,0:T(8,128)S(1)}, u32[]{:S(2)}, u32[]{:S(2)}) collective-permute-start(f32[4,128,128]{2,1,0:T(8,128)S(1)} %get-tuple-element.20), channel_id=1, source_target_pairs={{0,5},{1,6},{2,7},{4,9},{5,10},{6,11},{8,13},{9,14},{10,15},{12,17... | collective-permute-start | bytes 786440 | tf_op jit(solution)/shard_map/ppermute | solution.py:207
  134.1 20.4 %collective-permute-done.11 = f32[4,128,128]{2,1,0:T(8,128)S(1)} collective-permute-done((f32[4,128,128]{2,1,0:T(8,128)S(1)}, f32[4,128,128]{2,1,0:T(8,128)S(1)}, u32[]{:S(2)}, u32[]{:S(2)}) %collective-permute-start.11) | collective-permute-done | bytes 262176 | tf_op jit(solution)/shard_map/ppermute | solution.py:207
  154.6 4.2 %multiply_subtract_fusion = f32[4,384,384]{2,1,0:T(8,128)} fusion(f32[4,384,384]{2,1,0:T(8,128)} %copy-done.5, f32[4,128,128]{2,1,0:T(8,128)S(1)} %collective-permute-done.11, f32[4,128,384]{2,1,0:T(8,128)S(1)} %collective-permute-done.10, f32[4,384,384]{2,1,0:T(8,128)} %get-tuple-element.17, f32[4,384,128]{2,1,0:T(8,128)S(1)} %collective-permute-done.9), kind=kLoop, calls=%fused_computation | loop fusion | flops 2949120 | bytes 8912896 | tf_op jit(solution)/shard_map/sub | solution.py:235
  (31 shorter events, 2.0 us)
Async XLA Ops:
  0.0 13.0 %copy-start = (s32[1,4]{1,0:T(1,128)S(1)}, s32[1,4]{1,0:T(1,128)}, u32[]{:S(2)}) copy-start(s32[1,4]{1,0:T(1,128)} %param.13) | copy-start | bytes 52
  0.0 31.2 %copy-start.1 = (bf16[2,256,768]{2,1,0:T(8,128)(2,1)S(1)}, bf16[2,256,768]{2,1,0:T(8,128)(2,1)}, u32[]{:S(2)}) copy-start(bf16[2,256,768]{2,1,0:T(8,128)(2,1)} %constant.18.clone.ltab_ref) | copy-start | bytes 2359300
  0.0 31.2 %copy-start.2 = (bf16[2,768,256]{2,1,0:T(8,128)(2,1)S(1)}, bf16[2,768,256]{2,1,0:T(8,128)(2,1)}, u32[]{:S(2)}) copy-start(bf16[2,768,256]{2,1,0:T(8,128)(2,1)} %constant.17.clone.rtab_ref) | copy-start | bytes 2359300
  0.0 12.9 %copy-start.7 = (s32[8,2]{0,1:T(2,128)S(1)}, s32[8,2]{0,1:T(2,128)}, u32[]{:S(2)}) copy-start(s32[8,2]{0,1:T(2,128)} %param.12) | copy-start | bytes 196
  0.0 31.2 %copy-start.3 = (f32[8,128,128]{2,1,0:T(8,128)S(1)}, f32[8,128,128]{2,1,0:T(8,128)}, u32[]{:S(2)}) copy-start(f32[8,128,128]{2,1,0:T(8,128)} %meas_ref.3) | copy-start | bytes 1572868
  0.0 31.2 %copy-start.4 = (f32[2,128,128]{2,1,0:T(8,128)S(1)}, f32[2,128,128]{2,1,0:T(8,128)}, u32[]{:S(2)}) copy-start(f32[2,128,128]{2,1,0:T(8,128)} %probe_ref.3) | copy-start | bytes 393220
  2.3 27.9 %collective-permute-start = (f32[4,384,128]{2,1,0:T(8,128)}, f32[4,384,128]{2,1,0:T(8,128)S(1)}, u32[]{:S(2)}, u32[]{:S(2)}) collective-permute-start(f32[4,384,128]{2,1,0:T(8,128)} %slice.24), channel_id=1, source_target_pairs={{1,0},{2,1},{3,2},{5,4},{6,5},{7,6},{9,8},{10,9},{11,10},{13,12},{... | collective-permute-start | bytes 2359304 | tf_op jit(solution)/shard_map/ppermute | solution.py:207
  6.9 24.3 %collective-permute-start.1 = (f32[4,128,384]{2,1,0:T(8,128)}, f32[4,128,384]{2,1,0:T(8,128)}, u32[]{:S(2)}, u32[]{:S(2)}) collective-permute-start(f32[4,128,384]{2,1,0:T(8,128)} %slice.25), channel_id=1, source_target_pairs={{4,0},{5,1},{6,2},{7,3},{8,4},{9,5},{10,6},{11,7},{12,8},{13,9},{1... | collective-permute-start | bytes 2359304 | tf_op jit(solution)/shard_map/ppermute | solution.py:207
  10.9 19.2 %collective-permute-start.2 = (f32[4,128,128]{2,1,0:T(8,128)S(1)}, f32[4,128,128]{2,1,0:T(8,128)S(1)}, u32[]{:S(2)}, u32[]{:S(2)}) collective-permute-start(f32[4,128,128]{2,1,0:T(8,128)S(1)} %slice.26), channel_id=1, source_target_pairs={{5,0},{6,1},{7,2},{9,4},{10,5},{11,6},{13,8},{14,9},{15,10},{17,12... | collective-permute-start | bytes 786440 | tf_op jit(solution)/shard_map/ppermute | solution.py:207
  31.2 48.3 %copy-start.6 = (f32[2,2,384,384]{3,2,1,0:T(8,128)S(1)}, f32[2,2,384,384]{3,2,1,0:T(8,128)}, u32[]{:S(2)}) copy-start(f32[2,2,384,384]{3,2,1,0:T(8,128)} %param.8) | copy-start | bytes 7077892
  41.1 38.3 %collective-permute-start.3 = (f32[4,384,128]{2,1,0:T(8,128)S(1)}, f32[4,384,128]{2,1,0:T(8,128)S(1)}, u32[]{:S(2)}, u32[]{:S(2)}) collective-permute-start(f32[4,384,128]{2,1,0:T(8,128)S(1)} %get-tuple-element.14), channel_id=1, source_target_pairs={{0,1},{1,2},{2,3},{4,5},{5,6},{6,7},{8,9},{9,10},{10,11},{12,13},{... | collective-permute-start | bytes 2359304 | tf_op jit(solution)/shard_map/ppermute | solution.py:207
  51.8 27.7 %collective-permute-start.4 = (f32[4,128,384]{2,1,0:T(8,128)S(1)}, f32[4,128,384]{2,1,0:T(8,128)S(1)}, u32[]{:S(2)}, u32[]{:S(2)}) collective-permute-start(f32[4,128,384]{2,1,0:T(8,128)S(1)} %get-tuple-element.15), channel_id=1, source_target_pairs={{0,4},{1,5},{2,6},{3,7},{4,8},{5,9},{6,10},{7,11},{8,12},{9,13},{1... | collective-permute-start | bytes 2359304 | tf_op jit(solution)/shard_map/ppermute | solution.py:207
  56.5 23.0 %collective-permute-start.5 = (f32[4,128,128]{2,1,0:T(8,128)S(1)}, f32[4,128,128]{2,1,0:T(8,128)S(1)}, u32[]{:S(2)}, u32[]{:S(2)}) collective-permute-start(f32[4,128,128]{2,1,0:T(8,128)S(1)} %get-tuple-element.16), channel_id=1, source_target_pairs={{0,5},{1,6},{2,7},{4,9},{5,10},{6,11},{8,13},{9,14},{10,15},{12,17... | collective-permute-start | bytes 786440 | tf_op jit(solution)/shard_map/ppermute | solution.py:207
  81.6 23.9 %copy-start.5 = (f32[4,384,384]{2,1,0:T(8,128)}, f32[4,384,384]{2,1,0:T(8,128)S(1)}, u32[]{:S(2)}) copy-start(f32[4,384,384]{2,1,0:T(8,128)S(1)} %multiply_subtract_fusion.1.main_hbm) | copy-start | bytes 7077892
  81.7 23.8 %collective-permute-start.6 = (f32[4,384,128]{2,1,0:T(8,128)S(1)}, f32[4,384,128]{2,1,0:T(8,128)S(1)}, u32[]{:S(2)}, u32[]{:S(2)}) collective-permute-start(f32[4,384,128]{2,1,0:T(8,128)S(1)} %slice.27), channel_id=1, source_target_pairs={{1,0},{2,1},{3,2},{5,4},{6,5},{7,6},{9,8},{10,9},{11,10},{13,12},{... | collective-permute-start | bytes 2359304 | tf_op jit(solution)/shard_map/ppermute | solution.py:207
  83.6 21.9 %collective-permute-start.7 = (f32[4,128,384]{2,1,0:T(8,128)S(1)}, f32[4,128,384]{2,1,0:T(8,128)S(1)}, u32[]{:S(2)}, u32[]{:S(2)}) collective-permute-start(f32[4,128,384]{2,1,0:T(8,128)S(1)} %slice.28), channel_id=1, source_target_pairs={{4,0},{5,1},{6,2},{7,3},{8,4},{9,5},{10,6},{11,7},{12,8},{13,9},{1... | collective-permute-start | bytes 2359304 | tf_op jit(solution)/shard_map/ppermute | solution.py:207
  85.6 19.9 %collective-permute-start.8 = (f32[4,128,128]{2,1,0:T(8,128)S(1)}, f32[4,128,128]{2,1,0:T(8,128)S(1)}, u32[]{:S(2)}, u32[]{:S(2)}) collective-permute-start(f32[4,128,128]{2,1,0:T(8,128)S(1)} %slice.29), channel_id=1, source_target_pairs={{5,0},{6,1},{7,2},{9,4},{10,5},{11,6},{13,8},{14,9},{15,10},{17,12... | collective-permute-start | bytes 786440 | tf_op jit(solution)/shard_map/ppermute | solution.py:207
  115.1 39.4 %collective-permute-start.9 = (f32[4,384,128]{2,1,0:T(8,128)S(1)}, f32[4,384,128]{2,1,0:T(8,128)S(1)}, u32[]{:S(2)}, u32[]{:S(2)}) collective-permute-start(f32[4,384,128]{2,1,0:T(8,128)S(1)} %get-tuple-element.18), channel_id=1, source_target_pairs={{0,1},{1,2},{2,3},{4,5},{5,6},{6,7},{8,9},{9,10},{10,11},{12,13},{... | collective-permute-start | bytes 2359304 | tf_op jit(solution)/shard_map/ppermute | solution.py:207
  126.9 27.7 %collective-permute-start.10 = (f32[4,128,384]{2,1,0:T(8,128)S(1)}, f32[4,128,384]{2,1,0:T(8,128)S(1)}, u32[]{:S(2)}, u32[]{:S(2)}) collective-permute-start(f32[4,128,384]{2,1,0:T(8,128)S(1)} %get-tuple-element.19), channel_id=1, source_target_pairs={{0,4},{1,5},{2,6},{3,7},{4,8},{5,9},{6,10},{7,11},{8,12},{9,13},{1... | collective-permute-start | bytes 2359304 | tf_op jit(solution)/shard_map/ppermute | solution.py:207
  132.2 22.4 %collective-permute-start.11 = (f32[4,128,128]{2,1,0:T(8,128)S(1)}, f32[4,128,128]{2,1,0:T(8,128)S(1)}, u32[]{:S(2)}, u32[]{:S(2)}) collective-permute-start(f32[4,128,128]{2,1,0:T(8,128)S(1)} %get-tuple-element.20), channel_id=1, source_target_pairs={{0,5},{1,6},{2,7},{4,9},{5,10},{6,11},{8,13},{9,14},{10,15},{12,17... | collective-permute-start | bytes 786440 | tf_op jit(solution)/shard_map/ppermute | solution.py:207
where the time goes:
time: 159 us
  waiting for transfers between devices  75.8 us (48%)
  starting transfers between devices  49.5 us (31%)
  Pallas kernels  19.6 us (12%)
  local copies, waits for them, and re-layouts  7.34 us (5%)
  other arithmetic  6.29 us (4%)
    ppermute x12, waiting for transfers between devices, passed(): return lax.ppermute(x, ('row', 'col'), pairs)  75.8 us
    ppermute x12, starting transfers between devices, passed(): return lax.ppermute(x, ('row', 'col'), pairs)  49.5 us
    pallas_call x2, Pallas kernels, frame_grads(): pl.pallas_call(frames_kernel, out_shape=[jax.ShapeDtypeStruct((4, tile, t...  19.6 us
    sub x2, other arithmetic, local(): current = current - step_size * total  6.28 us
  transfers between devices with their start and end apart: 12, of which 5 were waited for; matrix products, arithmetic and copies ran while one was open for 3% of the time, Pallas kernels for 0%

commit v1 on v0

--- a/solution.py
+++ b/solution.py
@@ -78,19 +78,35 @@
     tile = main_hbm.shape[1]
     slots = meas_ref.shape[0]
     whole = tile + frame
+    has_right = lax.axis_index("col") < lax.axis_size("col") - 1
+    has_below = lax.axis_index("row") < lax.axis_size("row") - 1
+    core, rim = pl.ds(0, tile), pl.ds(tile, frame)
     copies = [
-        pltpu.make_async_copy(main_hbm, ext.at[:, pl.ds(0, tile), pl.ds(0, tile)], sems.at[0]),
-        pltpu.make_async_copy(right_hbm, ext.at[:, pl.ds(0, tile), pl.ds(tile, frame)], sems.at[1]),
-        pltpu.make_async_copy(below_hbm, ext.at[:, pl.ds(tile, frame), pl.ds(0, tile)], sems.at[2]),
-        pltpu.make_async_copy(
-            corner_hbm, ext.at[:, pl.ds(tile, frame), pl.ds(tile, frame)], sems.at[3]
+        (pltpu.make_async_copy(main_hbm, ext.at[:, core, core], sems.at[0]), True, core, core),
+        (pltpu.make_async_copy(right_hbm, ext.at[:, core, rim], sems.at[1]), has_right, core, rim),
+        (pltpu.make_async_copy(below_hbm, ext.at[:, rim, core], sems.at[2]), has_below, rim, core),
+        (
+            pltpu.make_async_copy(corner_hbm, ext.at[:, rim, rim], sems.at[3]),
+            has_right & has_below, rim, rim,
         ),
     ]
-    for copy in copies:
-        copy.start()
+    for copy, there, rows, cols in copies:
+        if there is True:
+            copy.start()
+            continue
+        pl.when(there)(copy.start)
+
+        @pl.when(jnp.logical_not(there))
+        def _():
+            part = ext.at[:, rows, cols]
+            part[...] = jnp.zeros(part.shape, jnp.float32)
+
     grad[...] = jnp.zeros_like(grad)
-    for copy in copies:
-        copy.wait()
+    for copy, there, rows, cols in copies:
+        if there is True:
+            copy.wait()
+        else:
+            pl.when(there)(copy.wait)
     count = counts_ref[0]
     lane = lax.broadcasted_iota(jnp.int32, (frame + SUB, frame), 1)
     sub = lax.broadcasted_iota(jnp.int32, (frame // SUB + 1, SUB, frame), 1)
@@ -196,15 +212,241 @@
     )(count, positions, main, right, below, corner, probe, kern, intensity, *tables)
 
 
-def passed(x, by_row, by_col):
-    rows, cols = lax.axis_size("row"), lax.axis_size("col")
-    pairs = [
-        (r * cols + c, (r + by_row) * cols + c + by_col)
-        for r in range(rows)
-        for c in range(cols)
-        if 0 <= r + by_row < rows and 0 <= c + by_col < cols
+MESH = pl.DeviceIdType.MESH
+
+
+class Around:
+    def __init__(self):
+        rows, cols = lax.axis_size("row"), lax.axis_size("col")
+        row, col = lax.axis_index("row"), lax.axis_index("col")
+        self.up = (lax.rem(row + rows - 1, rows), col)
+        self.down = (lax.rem(row + 1, rows), col)
+        self.left = (row, lax.rem(col + cols - 1, cols))
+        self.right = (row, lax.rem(col + 1, cols))
+        self.has_up = row > 0
+        self.has_down = row < rows - 1
+        self.has_left = col > 0
+        self.has_right = col < cols - 1
+
+    def meet(self):
+        barrier = pltpu.get_barrier_semaphore()
+        sides = (
+            (self.has_up, self.up),
+            (self.has_down, self.down),
+            (self.has_left, self.left),
+            (self.has_right, self.right),
+        )
+        for there, device in sides:
+
+            @pl.when(there)
+            def _():
+                pl.semaphore_signal(barrier, inc=1, device_id=device, device_id_type=MESH)
+
+        total = sum(there.astype(jnp.int32) for there, _ in sides)
+        pl.semaphore_wait(barrier, total)
+
+
+class Sends:
+    def __init__(self, send_sems, recv_sems):
+        self.send_sems, self.recv_sems = send_sems, recv_sems
+        self.copies = {}
+
+    def add(self, number, src, dst, device, has_target, has_source):
+        copy = pltpu.make_async_remote_copy(
+            src_ref=src,
+            dst_ref=dst,
+            send_sem=self.send_sems.at[number],
+            recv_sem=self.recv_sems.at[number],
+            device_id=device,
+            device_id_type=MESH,
+        )
+        self.copies[number] = (copy, has_target, has_source)
+
+    def start(self, number):
+        copy, has_target, _ = self.copies[number]
+        pl.when(has_target)(copy.start)
+
+    def arrived(self, number):
+        copy, _, has_source = self.copies[number]
+        pl.when(has_source)(copy.wait_recv)
+
+    def drain(self):
+        for copy, has_target, _ in self.copies.values():
+            pl.when(has_target)(copy.wait_send)
+
+
+def extend_kernel(main, right_out, below_out, corner_out, send_sems, recv_sems):
+    tile = main.shape[2]
+    frame = right_out.shape[2]
+    chunks = tile // frame
+    around = Around()
+    sends = Sends(send_sems, recv_sems)
+    for j in range(chunks):
+        part = pl.ds(j * frame, frame)
+        sends.add(
+            j, main.at[:, pl.ds(0, frame), part], below_out.at[:, :, part], around.up,
+            around.has_up, around.has_down,
+        )
+    sends.add(
+        chunks, main.at[:, :, pl.ds(0, frame)], right_out, around.left,
+        around.has_left, around.has_right,
+    )
+    sends.add(
+        chunks + 1, below_out.at[:, :, pl.ds(0, frame)], corner_out, around.left,
+        around.has_left & around.has_down, around.has_right & around.has_down,
+    )
+    around.meet()
+    for number in range(chunks + 1):
+        sends.start(number)
+    sends.arrived(0)
+    sends.start(chunks + 1)
+    for number in range(1, chunks + 2):
+        sends.arrived(number)
+    sends.drain()
+
+
+def fold_kernel(extend, main, g_main, g_right, g_below, g_corner, new, *rest):
+    if extend:
+        right_out, below_out, corner_out, *rest = rest
+    obj, own, head, low, in_right, in_below, in_corner, send_sems, recv_sems, sems = rest
+    tile = main.shape[2]
+    frame = g_corner.shape[2]
+    chunks = tile // frame
+    first, after = pl.ds(0, frame), pl.ds(frame, tile - frame)
+    parts = [pl.ds(j * frame, frame) for j in range(chunks)]
+    around = Around()
+    sends = Sends(send_sems, recv_sems)
+    corner_number, right_number, below_number = 0, 1, 2
+    sends.add(corner_number, g_corner, in_corner, around.right, around.has_right, around.has_left)
+    sends.add(right_number, g_right, in_right, around.right, around.has_right, around.has_left)
+    for j, part in enumerate(parts):
+        src = low if j == 0 else g_below.at[:, :, part]
+        sends.add(
+            below_number + j, src, in_below.at[:, :, part], around.down,
+            around.has_down, around.has_up,
+        )
+    rim_number = below_number + chunks
+    side_number = rim_number + chunks
+    if extend:
+        for j, part in enumerate(parts):
+            sends.add(
+                rim_number + j, new.at[:, first, part], below_out.at[:, :, part], around.up,
+                around.has_up, around.has_down,
+            )
+        for j, part in enumerate((first, after)):
+            sends.add(
+                side_number + j, new.at[:, part, first], right_out.at[:, part, :], around.left,
+                around.has_left, around.has_right,
+            )
+        sends.add(
+            side_number + 2, below_out.at[:, :, first], corner_out, around.left,
+            around.has_left & around.has_down, around.has_right & around.has_down,
+        )
+    loads = [
+        pltpu.make_async_copy(g_below.at[:, :, first], head, sems.at[0]),
+        pltpu.make_async_copy(main, obj, sems.at[1]),
+        pltpu.make_async_copy(g_main, own, sems.at[2]),
     ]
-    return lax.ppermute(x, ("row", "col"), pairs)
+    for load in loads:
+        load.start()
+
+    @pl.when(jnp.logical_not(around.has_left))
+    def _():
+        in_right[...] = jnp.zeros_like(in_right)
+        in_corner[...] = jnp.zeros_like(in_corner)
+
+    @pl.when(jnp.logical_not(around.has_up))
+    def _():
+        in_below[...] = jnp.zeros_like(in_below)
+
+    around.meet()
+    sends.start(corner_number)
+    sends.start(right_number)
+    for j in range(1, chunks):
+        sends.start(below_number + j)
+    loads[0].wait()
+    sends.arrived(corner_number)
+    low[...] = head[...] + in_corner[...]
+    sends.start(below_number)
+    loads[1].wait()
+    loads[2].wait()
+    new[:, after, after] = obj[:, after, after] - step_size * own[:, after, after]
+    sends.arrived(right_number)
+    new[:, after, first] = obj[:, after, first] - step_size * (
+        own[:, after, first] + in_right[:, after, :]
+    )
+    if extend:
+        sends.start(side_number + 1)
+    order = [1, 0] + list(range(2, chunks)) if chunks > 1 else [0]
+    for j in order:
+        part = parts[j]
+        sends.arrived(below_number + j)
+        total = own[:, first, part] + in_below[:, :, part]
+        if j == 0:
+            total = total + in_right[:, first, :]
+        new[:, first, part] = obj[:, first, part] - step_size * total
+        if extend:
+            sends.start(rim_number + j)
+            if j == 0:
+                sends.start(side_number)
+    if extend:
+        sends.arrived(rim_number)
+        sends.start(side_number + 2)
+        for j in range(1, chunks):
+            sends.arrived(rim_number + j)
+        for number in range(side_number, side_number + 3):
+            sends.arrived(number)
+    sends.drain()
+
+
+def extend_call(main, frame):
+    tile = main.shape[2]
+    anywhere = pl.BlockSpec(memory_space=pl.ANY)
+    copies = tile // frame + 2
+    return pl.pallas_call(
+        extend_kernel,
+        out_shape=rim_shapes(tile, frame),
+        in_specs=[anywhere],
+        out_specs=[anywhere] * 3,
+        scratch_shapes=[pltpu.SemaphoreType.DMA((copies,)), pltpu.SemaphoreType.DMA((copies,))],
+        compiler_params=pltpu.CompilerParams(collective_id=0, has_side_effects=True),
+    )(main)
+
+
+def rim_shapes(tile, frame):
+    shapes = ((4, tile, frame), (4, frame, tile), (4, frame, frame))
+    return [jax.ShapeDtypeStruct(shape, jnp.float32) for shape in shapes]
+
+
+def fold_call(main, grads, extend):
+    tile = main.shape[2]
+    frame = grads[3].shape[2]
+    anywhere = pl.BlockSpec(memory_space=pl.ANY)
+    vmem = pl.BlockSpec(memory_space=pltpu.VMEM)
+    copies = 2 * (tile // frame) + 5
+    outs = [jax.ShapeDtypeStruct(main.shape, jnp.float32)]
+    block = pltpu.VMEM((4, frame, frame), jnp.float32)
+    return pl.pallas_call(
+        functools.partial(fold_kernel, extend),
+        out_shape=outs + (rim_shapes(tile, frame) if extend else []),
+        in_specs=[anywhere] * 5,
+        out_specs=[vmem] + ([anywhere] * 3 if extend else []),
+        scratch_shapes=[
+            pltpu.VMEM(main.shape, jnp.float32),
+            pltpu.VMEM(main.shape, jnp.float32),
+            block,
+            block,
+            pltpu.VMEM((4, tile, frame), jnp.float32),
+            pltpu.VMEM((4, frame, tile), jnp.float32),
+            block,
+            pltpu.SemaphoreType.DMA((copies,)),
+            pltpu.SemaphoreType.DMA((copies,)),
+            pltpu.SemaphoreType.DMA((3,)),
+        ],
+        compiler_params=pltpu.CompilerParams(
+            collective_id=1 if extend else 2, has_side_effects=True, vmem_limit_bytes=32 << 20
+        ),
+    )(main, *grads)
 
 
 def local(object_tiles, probe_field, prop_phase, intensity, positions, counts):
@@ -215,24 +457,10 @@
     count = lax.dynamic_slice(counts[0], (lax.axis_index("col"),), (1,))
     flat = positions.reshape(-1)
     current = object_tiles.reshape(4, tile, tile)
+    rims = extend_call(current, frame)
     for iteration in range(ITERS):
-        right = passed(current[:, :, :frame], 0, -1)
-        below = passed(current[:, :frame, :], -1, 0)
-        corner = passed(current[:, :frame, :frame], -1, -1)
-        g_main, g_right, g_below, g_corner = frame_grads(
-            count, flat, current, right, below, corner, probe_field, kern, intensity, tables
-        )
-        g_right = passed(g_right, 0, 1)
-        g_below = passed(g_below, 1, 0)
-        g_corner = passed(g_corner, 1, 1)
-        rest = tile - frame
-        total = (
-            g_main
-            + jnp.pad(g_right, ((0, 0), (0, 0), (0, rest)))
-            + jnp.pad(g_below, ((0, 0), (0, rest), (0, 0)))
-            + jnp.pad(g_corner, ((0, 0), (0, rest), (0, rest)))
-        )
-        current = current - step_size * total
+        grads = frame_grads(count, flat, current, *rims, probe_field, kern, intensity, tables)
+        current, *rims = fold_call(current, grads, iteration < ITERS - 1)
     return current.reshape(object_tiles.shape)
 
 

time: 159 us -> 135 us (0.85); the launches traced: 159 us -> 133 us
  Pallas kernels: 19.6 us -> 120 us
  waiting for transfers between devices: 75.8 us -> 0 us
  starting transfers between devices: 49.5 us -> 0 us
  other arithmetic: 6.29 us -> 0.01 us
  local copies, waits for them, and re-layouts: 7.34 us -> 12.5 us
    pallas_call x0 -> x3, Pallas kernels: none -> 101 us  [the longest x2 80.1 us: fold_call(): pl.pallas_call(functools.partial(fold_kernel, extend), out_shape=outs + (...]
    ppermute x12 -> x0, waiting for transfers between devices: 75.8 us -> none  [passed(): return lax.ppermute(x, ('row', 'col'), pairs)]
    ppermute x12 -> x0, starting transfers between devices: 49.5 us -> none  [passed(): return lax.ppermute(x, ('row', 'col'), pairs)]
    unnamed x17 -> x28, local copies, waits for them, and re-layouts: 0.12 us -> 10.7 us
    sub x2 -> x0, other arithmetic: 6.28 us -> none  [local(): current = current - step_size * total]
    slice x6 -> x0, local copies, waits for them, and re-layouts: 5.4 us -> none  [the longest x2 2.27 us: local(): right = passed(current[:, :, :frame], 0, -1)]
  transfers between devices with their start and end apart: 12 -> 0, of which waited for: 5 -> 0; matrix products, arithmetic and copies ran while one was open for 3% -> 0% of each run, Pallas kernels for 0% -> 0%
where the time goes in v1:
time: 135 us; the launch traced here: 133 us
  Pallas kernels  120 us (89%)
  local copies, waits for them, and re-layouts  12.5 us (9%)
    pallas_call x2, Pallas kernels, fold_call(): pl.pallas_call(functools.partial(fold_kernel, extend), out_shape=outs + (...  80.1 us
    pallas_call x1, Pallas kernels, extend_call(): pl.pallas_call(extend_kernel, out_shape=rim_shapes(tile, frame), in_specs...  21 us
    pallas_call x2, Pallas kernels, frame_grads(): pl.pallas_call(frames_kernel, out_shape=[jax.ShapeDtypeStruct((4, tile, t...  19.2 us
    unnamed x28, local copies, waits for them, and re-layouts  10.7 us

profile of v1, /device:TPU:9, one launch (start us, length us, event | category | flops | bytes accessed | tf_op | source)
XLA Modules:
  0.0 133.0 jit_solution(1489522847566544543)
XLA Ops:
  0.0 0.6 copy-done
  0.7 0.6 constant_dynamic-slice_fusion
  1.2 0.8 copy.10
  2.0 0.1 reshape.11.pos_ref
  2.1 1.1 cosine_bitcast_fusion
  3.2 21.0 %shard_map.82 = (f32[4,384,128]{2,1,0:T(8,128)}, f32[4,128,384]{2,1,0:T(8,128)}, f32[4,128,128]{2,1,0:T(8,128)}) custom-call(f32[4,384,384]{2,1,0:T(8,128)} %bitcast.7), custom_call_target="tpu_custom_call" | custom-call | tf_op jit(solution)/shard_map/pallas_call | solution.py:406
  24.1 0.0 copy-done.4
  24.1 0.0 copy-done.5
  24.2 0.0 copy-done.8
  24.2 0.0 copy-done.11
  24.2 0.0 copy-start.9
  24.2 1.1 copy-done.9
  25.3 1.1 copy-done.10
  26.4 0.9 copy-done.12
  27.4 9.6 %shard_map.83 = (f32[4,384,384]{2,1,0:T(8,128)}, f32[4,384,128]{2,1,0:T(8,128)S(1)}, f32[4,128,384]{2,1,0:T(8,128)S(1)}, f32[4,128,128]{2,1,0:T(8,128)S(1)}) custom-call(s32[1]{0:T(128)} %bitcast.1.counts_ref, s32[16]{0:T(128)S(1)} %reshape.11.pos_ref, f32[4,384,384]{2,1,0:T(8,128)} %bitcast.8, f32[4,384,128]{2,1,0:T(8,128)S(1)} %copy-done.9, ...), custom_call_target="tpu_custom_call" | custom-call | tf_op jit(solution)/shard_map/pallas_call | solution.py:196
  37.0 0.0 copy-start.6
  37.0 1.7 %copy-done.6 = f32[4,384,384]{2,1,0:T(8,128)S(1)} copy-done((f32[4,384,384]{2,1,0:T(8,128)S(1)}, f32[4,384,384]{2,1,0:T(8,128)}, u32[]{:S(2)}) %copy-start.6) | copy-done | bytes 2359320
  38.7 55.7 %shard_map.84 = (f32[4,384,384]{2,1,0:T(8,128)S(1)}, f32[4,384,128]{2,1,0:T(8,128)S(1)}, f32[4,128,384]{2,1,0:T(8,128)S(1)}, f32[4,128,128]{2,1,0:T(8,128)S(1)}) custom-call(f32[4,384,384]{2,1,0:T(8,128)S(1)} %bitcast.9, f32[4,384,384]{2,1,0:T(8,128)S(1)} %copy-done.6, f32[4,384,128]{2,1,0:T(8,128)S(1)} %get-tuple-element.24.g_right, ...), custom_call_target="tpu_custom_call" | custom-call | tf_op jit(solution)/shard_map/pallas_call | solution.py:429
  94.4 0.0 copy-start.2
  94.4 1.4 %copy-done.2 = f32[4,384,384]{2,1,0:T(8,128)} copy-done((f32[4,384,384]{2,1,0:T(8,128)}, f32[4,384,384]{2,1,0:T(8,128)S(1)}, u32[]{:S(2)}) %copy-start.2) | copy-done | bytes 2359320
  95.8 9.6 %shard_map.85 = (f32[4,384,384]{2,1,0:T(8,128)}, f32[4,384,128]{2,1,0:T(8,128)S(1)}, f32[4,128,384]{2,1,0:T(8,128)S(1)}, f32[4,128,128]{2,1,0:T(8,128)S(1)}) custom-call(s32[1]{0:T(128)} %bitcast.1.counts_ref, s32[16]{0:T(128)S(1)} %reshape.11.pos_ref, f32[4,384,384]{2,1,0:T(8,128)} %copy-done.2, f32[4,384,128]{2,1,0:T(8,128)S(1)} %get-tuple-element.28.right_hbm, ...), custom_call_target="tpu_custom_call" | custom-call | tf_op jit(solution)/shard_map/pallas_call | solution.py:196
  105.5 1.7 %copy-done.7 = f32[4,384,384]{2,1,0:T(8,128)S(1)} copy-done((f32[4,384,384]{2,1,0:T(8,128)S(1)}, f32[4,384,384]{2,1,0:T(8,128)}, u32[]{:S(2)}) %copy-start.7) | copy-done | bytes 2359320
  107.1 24.4 %shard_map.86 = f32[4,384,384]{2,1,0:T(8,128)S(1)} custom-call(f32[4,384,384]{2,1,0:T(8,128)S(1)} %copy-done.3, f32[4,384,384]{2,1,0:T(8,128)S(1)} %copy-done.7, f32[4,384,128]{2,1,0:T(8,128)S(1)} %get-tuple-element.32.g_right, f32[4,128,384]{2,1,0:T(8,128)S(1)} %get-tuple-element.33.g_below, f32[4,128,128]{2,1,0:T(8,128)S(1)} %get-tuple-element.34.g_corner), custom_call_target="tpu_custom_call" | custom-call | tf_op jit(solution)/shard_map/pallas_call | solution.py:429
  131.6 1.4 %copy.12 = f32[2,2,384,384]{3,2,1,0:T(8,128)} copy(f32[2,2,384,384]{3,2,1,0:T(8,128)S(1)} %bitcast.10) | data formatting | bytes 4718592
  (13 shorter events, 0.0 us)
Async XLA Ops:
  0.0 0.7 copy-start
  0.0 24.1 %copy-start.4 = (bf16[2,256,768]{2,1,0:T(8,128)(2,1)S(1)}, bf16[2,256,768]{2,1,0:T(8,128)(2,1)}, u32[]{:S(2)}) copy-start(bf16[2,256,768]{2,1,0:T(8,128)(2,1)} %constant.14.clone.ltab_ref) | copy-start | bytes 2359300
  0.0 24.1 %copy-start.5 = (bf16[2,768,256]{2,1,0:T(8,128)(2,1)S(1)}, bf16[2,768,256]{2,1,0:T(8,128)(2,1)}, u32[]{:S(2)}) copy-start(bf16[2,768,256]{2,1,0:T(8,128)(2,1)} %constant.13.clone.rtab_ref) | copy-start | bytes 2359300
  0.0 24.1 %copy-start.8 = (f32[8,128,128]{2,1,0:T(8,128)S(1)}, f32[8,128,128]{2,1,0:T(8,128)}, u32[]{:S(2)}) copy-start(f32[8,128,128]{2,1,0:T(8,128)} %meas_ref.3) | copy-start | bytes 1572868
  0.0 24.1 %copy-start.11 = (f32[2,128,128]{2,1,0:T(8,128)S(1)}, f32[2,128,128]{2,1,0:T(8,128)}, u32[]{:S(2)}) copy-start(f32[2,128,128]{2,1,0:T(8,128)} %probe_ref.3) | copy-start | bytes 393220
  24.2 1.1 copy-start.9
  25.3 1.1 copy-start.10
  26.4 0.9 copy-start.12
  27.4 9.6 %copy-start.1 = (f32[2,2,384,384]{3,2,1,0:T(8,128)S(1)}, f32[2,2,384,384]{3,2,1,0:T(8,128)}, u32[]{:S(2)}) copy-start(f32[2,2,384,384]{3,2,1,0:T(8,128)} %param.8) | copy-start | bytes 7077892
  37.0 1.7 %copy-start.6 = (f32[4,384,384]{2,1,0:T(8,128)S(1)}, f32[4,384,384]{2,1,0:T(8,128)}, u32[]{:S(2)}) copy-start(f32[4,384,384]{2,1,0:T(8,128)} %get-tuple-element.23.g_main) | copy-start | bytes 7077892
  94.4 1.4 %copy-start.2 = (f32[4,384,384]{2,1,0:T(8,128)}, f32[4,384,384]{2,1,0:T(8,128)S(1)}, u32[]{:S(2)}) copy-start(f32[4,384,384]{2,1,0:T(8,128)S(1)} %get-tuple-element.27.main_hbm.main) | copy-start | bytes 7077892
  95.8 9.7 %copy-start.3 = (f32[4,384,384]{2,1,0:T(8,128)S(1)}, f32[4,384,384]{2,1,0:T(8,128)}, u32[]{:S(2)}) copy-start(f32[4,384,384]{2,1,0:T(8,128)} %copy-done.2) | copy-start | bytes 7077892
  105.5 1.7 %copy-start.7 = (f32[4,384,384]{2,1,0:T(8,128)S(1)}, f32[4,384,384]{2,1,0:T(8,128)}, u32[]{:S(2)}) copy-start(f32[4,384,384]{2,1,0:T(8,128)} %get-tuple-element.31.g_main) | copy-start | bytes 7077892

commit v2 on v1

v2 whole, which is shorter than its diff:
```python
import functools

import jax
import jax.numpy as jnp
import numpy as np
from jax import lax
from jax.experimental import pallas as pl
from jax.experimental.pallas import tpu as pltpu
from jax.sharding import PartitionSpec as P

ITERS = 2
GROUP = 4
SUB = 8

step_size = 0.2


def dft_tables(size):
    index = np.arange(size)
    phase = (index[:, None] * index[None, :] % size) * (2.0 * np.pi / size)
    re = np.cos(phase) / np.sqrt(size)
    im = -np.sin(phase) / np.sqrt(size)
    rights, lefts = [], []
    for sign in (1.0, -1.0):
        right = np.block([[re, sign * im], [-sign * im, re]]).astype(np.float32)
        high = right.astype(jnp.bfloat16)
        low = (right - high.astype(np.float32)).astype(jnp.bfloat16)
        rights.append(np.concatenate([high, high, low], axis=0))
        lefts.append(np.concatenate([high.T, high.T, low.T], axis=1))
    return np.stack(rights), np.stack(lefts)


def split(x):
    high = x.astype(jnp.bfloat16)
    low = (x - high.astype(jnp.float32)).astype(jnp.bfloat16)
    return high, low


def by_right(waves, table):
    size = waves[0][0].shape[0]
    x = jnp.concatenate([jnp.concatenate(wave, axis=1) for wave in waves], axis=0)
    high, low = split(x)
    y = jnp.dot(
        jnp.concatenate([high, low, high], axis=1), table, preferred_element_type=jnp.float32
    )
    return [
        (y[i * size : (i + 1) * size, :size], y[i * size : (i + 1) * size, size:])
        for i in range(len(waves))
    ]


def by_left(waves, table):
    size = waves[0][0].shape[0]
    x = jnp.concatenate([jnp.concatenate(wave, axis=0) for wave in waves], axis=1)
    high, low = split(x)
    y = jnp.dot(
        table, jnp.concatenate([high, low, high], axis=0), preferred_element_type=jnp.float32
    )
    return [
        (y[:size, i * size : (i + 1) * size], y[size:, i * size : (i + 1) * size])
        for i in range(len(waves))
    ]


def mul(a, b):
    return (a[0] * b[0] - a[1] * b[1], a[0] * b[1] + a[1] * b[0])


def conj_mul(a, b):
    return (a[0] * b[0] + a[1] * b[1], a[0] * b[1] - a[1] * b[0])


def frames_kernel(
    counts_ref, pos_ref, ext, probe_ref, kern_ref, meas_ref, rtab_ref, ltab_ref, grad,
):
    frame = probe_ref.shape[1]
    slots = meas_ref.shape[0]
    grad[...] = jnp.zeros_like(grad)
    count = counts_ref[0, lax.axis_index("col")]
    lane = lax.broadcasted_iota(jnp.int32, (frame + SUB, frame), 1)
    sub = lax.broadcasted_iota(jnp.int32, (frame // SUB + 1, SUB, frame), 1)
    edge = jnp.zeros((1, SUB, frame), jnp.float32)

    @pl.loop(0, (count + GROUP - 1) // GROUP)
    def _(group):
        places, firsts, seconds = [], [], []
        for i in range(GROUP):
            slot = group * GROUP + i
            here = jnp.minimum(slot, slots - 1)
            weight = (slot < count).astype(jnp.float32)
            top = pos_ref[here, 0]
            left = pos_ref[here, 1]
            block = left // frame
            shift = left - block * frame
            near = pl.ds(pl.multiple_of(block * frame, frame), frame)
            far = pl.ds(pl.multiple_of(block * frame + frame, frame), frame)
            start = top // SUB * SUB
            drop = top - start
            rows = pl.ds(pl.multiple_of(start, SUB), frame + SUB)
            back = lax.rem(frame - shift, frame)
            lift = lax.rem(SUB - drop, SUB)
            planes = []
            for s in range(4):
                a = pltpu.roll(ext[s, rows, near], back, 1)
                b = pltpu.roll(ext[s, rows, far], back, 1)
                wide = jnp.where(lane < frame - shift, a, b).reshape(-1, SUB, frame)
                wide = pltpu.roll(wide, lift, 1)
                plane = jnp.where(sub[1:] < SUB - drop, wide[:-1], wide[1:])
                planes.append(plane.reshape(frame, frame))
            places.append((here, weight, rows, near, far, shift, drop))
            firsts.append((planes[0], planes[1]))
            seconds.append((planes[2], planes[3]))
        probe = (probe_ref[0], probe_ref[1])
        kern = (kern_ref[0], kern_ref[1])
        lit = [mul(probe, first) for first in firsts]
        freq = by_left(by_right(lit, rtab_ref[0]), ltab_ref[0])
        moved = [mul(kern, f) for f in freq]
        inner = by_right(by_left(moved, ltab_ref[1]), rtab_ref[1])
        leave = [mul(b, o) for b, o in zip(inner, seconds)]
        far_field = by_left(by_right(leave, rtab_ref[0]), ltab_ref[0])
        missed = []
        for place, (re, im) in zip(places, far_field):
            misfit = re * re + im * im - meas_ref[place[0]]
            missed.append((misfit * re, misfit * im))
        back_wave = by_right(by_left(missed, ltab_ref[1]), rtab_ref[1])
        grad_two = [conj_mul(b, g) for b, g in zip(inner, back_wave)]
        carry = [conj_mul(o, g) for o, g in zip(seconds, back_wave)]
        carried = by_left(by_right(carry, rtab_ref[0]), ltab_ref[0])
        unmoved = [conj_mul(kern, f) for f in carried]
        near_wave = by_right(by_left(unmoved, ltab_ref[1]), rtab_ref[1])
        grad_one = [conj_mul(probe, w) for w in near_wave]
        for place, one, two in zip(places, grad_one, grad_two):
            here, weight, rows, near, far, shift, drop = place
            for s, value in enumerate((one[0], one[1], two[0], two[1])):
                turned = pltpu.roll(value * weight, shift, 1).reshape(-1, SUB, frame)
                turned = pltpu.roll(turned, drop, 1)
                upper = jnp.concatenate([turned, edge], axis=0)
                lower = jnp.concatenate([edge, turned], axis=0)
                turned = jnp.where(sub >= drop, upper, lower).reshape(frame + SUB, frame)
                inside = lane >= shift
                grad[s, rows, near] += jnp.where(inside, turned, 0.0)
                grad[s, rows, far] += jnp.where(inside, 0.0, turned)


def frame_grads(counts, positions, ext, probe, kern, intensity, tables):
    smem = pl.BlockSpec(memory_space=pltpu.SMEM)
    vmem = pl.BlockSpec(memory_space=pltpu.VMEM)
    return pl.pallas_call(
        frames_kernel,
        out_shape=jax.ShapeDtypeStruct(ext.shape, jnp.float32),
        in_specs=[smem, smem] + [vmem] * 6,
        out_specs=vmem,
        compiler_params=pltpu.CompilerParams(vmem_limit_bytes=40 << 20),
    )(counts, positions, ext, probe, kern, intensity, *tables)


MESH = pl.DeviceIdType.MESH


class Around:
    def __init__(self):
        rows, cols = lax.axis_size("row"), lax.axis_size("col")
        row, col = lax.axis_index("row"), lax.axis_index("col")
        self.up = (lax.rem(row + rows - 1, rows), col)
        self.down = (lax.rem(row + 1, rows), col)
        self.left = (row, lax.rem(col + cols - 1, cols))
        self.right = (row, lax.rem(col + 1, cols))
        self.has_up = row > 0
        self.has_down = row < rows - 1
        self.has_left = col > 0
        self.has_right = col < cols - 1

    def meet(self):
        barrier = pltpu.get_barrier_semaphore()
        sides = (
            (self.has_up, self.up),
            (self.has_down, self.down),
            (self.has_left, self.left),
            (self.has_right, self.right),
        )
        for there, device in sides:

            @pl.when(there)
            def _():
                pl.semaphore_signal(barrier, inc=1, device_id=device, device_id_type=MESH)

        total = sum(there.astype(jnp.int32) for there, _ in sides)
        pl.semaphore_wait(barrier, total)


class Sends:
    def __init__(self, send_sems, recv_sems):
        self.send_sems, self.recv_sems = send_sems, recv_sems
        self.copies = {}

    def add(self, number, src, dst, device, has_target, has_source):
        copy = pltpu.make_async_remote_copy(
            src_ref=src,
            dst_ref=dst,
            send_sem=self.send_sems.at[number],
            recv_sem=self.recv_sems.at[number],
            device_id=device,
            device_id_type=MESH,
        )
        self.copies[number] = (copy, has_target, has_source)

    def start(self, number):
        copy, has_target, _ = self.copies[number]
        pl.when(has_target)(copy.start)

    def arrived(self, number):
        copy, _, has_source = self.copies[number]
        pl.when(has_source)(copy.wait_recv)

    def drain(self):
        for copy, has_target, _ in self.copies.values():
            pl.when(has_target)(copy.wait_send)


def extend_kernel(main, phase, ext, kern, send_sems, recv_sems, sem):
    tile = main.shape[2]
    frame = phase.shape[0]
    chunks = tile // frame
    core, rim, first = pl.ds(0, tile), pl.ds(tile, frame), pl.ds(0, frame)
    around = Around()
    sends = Sends(send_sems, recv_sems)
    for j in range(chunks):
        part = pl.ds(j * frame, frame)
        sends.add(
            j, main.at[:, first, part], ext.at[:, rim, part], around.up,
            around.has_up, around.has_down,
        )
    sends.add(
        chunks, main.at[:, :, first], ext.at[:, core, rim], around.left,
        around.has_left, around.has_right,
    )
    sends.add(
        chunks + 1, ext.at[:, rim, first], ext.at[:, rim, rim], around.left,
        around.has_left & around.has_down, around.has_right & around.has_down,
    )
    around.meet()
    for number in range(chunks + 1):
        sends.start(number)
    load = pltpu.make_async_copy(main, ext.at[:, core, core], sem)
    load.start()
    kern[0] = jnp.cos(phase[...])
    kern[1] = jnp.sin(phase[...])
    clear_edges(around, ext, tile, frame)
    sends.arrived(0)
    sends.start(chunks + 1)
    load.wait()
    for number in range(1, chunks + 2):
        sends.arrived(number)
    sends.drain()


def clear_edges(around, ext, tile, frame):
    @pl.when(jnp.logical_not(around.has_right))
    def _():
        ext[:, :tile, tile:] = jnp.zeros((4, tile, frame), jnp.float32)

    @pl.when(jnp.logical_not(around.has_down))
    def _():
        ext[:, tile:, :tile] = jnp.zeros((4, frame, tile), jnp.float32)

    @pl.when(jnp.logical_not(around.has_right & around.has_down))
    def _():
        ext[:, tile:, tile:] = jnp.zeros((4, frame, frame), jnp.float32)


def fold_kernel(extend, tile, frame, ext, grad, new, *rest):
    if extend:
        in_top, high, *rest = rest
    low, in_right, in_below, in_corner, send_sems, recv_sems = rest
    chunks = tile // frame
    core, rim = pl.ds(0, tile), pl.ds(tile, frame)
    first, after = pl.ds(0, frame), pl.ds(frame, tile - frame)
    parts = [pl.ds(j * frame, frame) for j in range(chunks)]
    around = Around()
    sends = Sends(send_sems, recv_sems)
    corner_no, side_no, below_no = 0, 1, 3
    top_no = below_no + chunks
    rim_no = top_no + chunks
    there, source = around.has_right, around.has_left
    sends.add(corner_no, grad.at[:, rim, rim], in_corner, around.right, there, source)
    for j, part in enumerate((first, after)):
        sends.add(
            side_no + j, grad.at[:, part, rim], in_right.at[:, part, :], around.right, there, source
        )
    for j, part in enumerate(parts):
        sends.add(
            below_no + j, low if j == 0 else grad.at[:, rim, part], in_below.at[:, :, part],
            around.down, around.has_down, around.has_up,
        )
        if extend:
            sends.add(
                top_no + j, high if j == 0 else grad.at[:, first, part], in_top.at[:, :, part],
                around.up, around.has_up, around.has_down,
            )
    if extend:
        for j, part in enumerate((first, after)):
            sends.add(
                rim_no + j, new.at[:, part, first], new.at[:, part, rim], around.left,
                around.has_left, around.has_right,
            )
        sends.add(
            rim_no + 2, new.at[:, rim, first], new.at[:, rim, rim], around.left,
            around.has_left & around.has_down, around.has_right & around.has_down,
        )

    around.meet()

    def start_row(j):
        sends.start(below_no + j)
        if extend:
            sends.start(top_no + j)

    sends.start(corner_no)
    sends.start(side_no)
    if chunks > 1:
        start_row(1)
        sends.start(side_no + 1)

    @pl.when(jnp.logical_not(around.has_left))
    def _():
        in_right[...] = jnp.zeros_like(in_right)
        in_corner[...] = jnp.zeros_like(in_corner)

    @pl.when(jnp.logical_not(around.has_up))
    def _():
        in_below[...] = jnp.zeros_like(in_below)

    if extend:
        clear_edges(around, new, tile, frame)
    sends.arrived(corner_no)
    low[...] = grad[:, rim, first] + in_corner[...]
    sends.start(below_no)
    sends.arrived(side_no)
    if extend:
        high[...] = grad[:, first, first] + in_right[:, first, :]
        sends.start(top_no)
    for j in range(2, chunks):
        start_row(j)
    new[:, after, after] = ext[:, after, after] - step_size * grad[:, after, after]
    if chunks > 1:
        sends.arrived(side_no + 1)
        new[:, after, first] = ext[:, after, first] - step_size * (
            grad[:, after, first] + in_right[:, after, :]
        )
        if extend:
            sends.start(rim_no + 1)
    order = [1, 0] + list(range(2, chunks)) if chunks > 1 else [0]
    for j in order:
        part = parts[j]
        sends.arrived(below_no + j)
        total = grad[:, first, part] + in_below[:, :, part]
        if j == 0:
            total = total + in_right[:, first, :]
        new[:, first, part] = ext[:, first, part] - step_size * total
        if extend:
            if j == 0:
                sends.start(rim_no)
            sends.arrived(top_no + j)

            @pl.when(around.has_down)
            def _():
                own = low[...] if j == 0 else grad[:, rim, part]
                new[:, rim, part] = ext[:, rim, part] - step_size * (own + in_top[:, :, part])

            if j == 0:
                sends.start(rim_no + 2)
    if extend:
        for number in range(rim_no, rim_no + 3):
            if chunks > 1 or number != rim_no + 1:
                sends.arrived(number)
    sends.drain()


def extend_call(main, phase):
    tile, frame = main.shape[2], phase.shape[0]
    anywhere = pl.BlockSpec(memory_space=pl.ANY)
    vmem = pl.BlockSpec(memory_space=pltpu.VMEM)
    copies = tile // frame + 2
    whole = tile + frame
    return pl.pallas_call(
        extend_kernel,
        out_shape=[
            jax.ShapeDtypeStruct((4, whole, whole), jnp.float32),
            jax.ShapeDtypeStruct((2, frame, frame), jnp.float32),
        ],
        in_specs=[anywhere, vmem],
        out_specs=[vmem] * 2,
        scratch_shapes=[
            pltpu.SemaphoreType.DMA((copies,)),
            pltpu.SemaphoreType.DMA((copies,)),
            pltpu.SemaphoreType.DMA,
        ],
        compiler_params=pltpu.CompilerParams(
            collective_id=0, has_side_effects=True, vmem_limit_bytes=16 << 20
        ),
    )(main, phase)


def fold_call(ext, grad, frame, extend):
    whole = ext.shape[2]
    tile = whole - frame
    vmem = pl.BlockSpec(memory_space=pltpu.VMEM)
    copies = 2 * (tile // frame) + 6
    side = whole if extend else tile
    block = pltpu.VMEM((4, frame, frame), jnp.float32)
    strip = pltpu.VMEM((4, frame, tile), jnp.float32)
    return pl.pallas_call(
        functools.partial(fold_kernel, extend, tile, frame),
        out_shape=jax.ShapeDtypeStruct((4, side, side), jnp.float32),
        in_specs=[vmem] * 2,
        out_specs=vmem,
        scratch_shapes=([strip, block] if extend else [])
        + [
            block,
            pltpu.VMEM((4, tile, frame), jnp.float32),
            strip,
            block,
            pltpu.SemaphoreType.DMA((copies,)),
            pltpu.SemaphoreType.DMA((copies,)),
        ],
        compiler_params=pltpu.CompilerParams(
            collective_id=1 if extend else 2, has_side_effects=True, vmem_limit_bytes=32 << 20
        ),
    )(ext, grad)


def local(object_tiles, probe_field, prop_phase, intensity, positions, counts):
    tile = object_tiles.shape[3]
    frame = probe_field.shape[1]
    tables = [jnp.asarray(t) for t in dft_tables(frame)]
    ext, kern = extend_call(object_tiles.reshape(4, tile, tile), prop_phase)
    for iteration in range(ITERS):
        grad = frame_grads(counts, positions, ext, probe_field, kern, intensity, tables)
        ext = fold_call(ext, grad, frame, iteration < ITERS - 1)
    return ext.reshape(object_tiles.shape)


def solution(mesh):
    return jax.shard_map(
        local,
        mesh=mesh,
        in_specs=(
            P(None, None, "row", "col"),
            P(),
            P(),
            P(("row", "col"), None, None),
            P(("row", "col"), None),
            P("row", None),
        ),
        out_specs=P(None, None, "row", "col"),
        check_vma=False,
    )
```

time: 135 us -> 112 us (0.83)
  Pallas kernels: 120 us -> 101 us
  local copies, waits for them, and re-layouts: 12.5 us -> 9.55 us
    pallas_call x5, Pallas kernels: 120 us -> 101 us  [the longest x2 57.6 us: fold_call(): pl.pallas_call(functools.partial(fold_kernel, extend, tile, frame), out_s...]
    unnamed x28 -> x24, local copies, waits for them, and re-layouts: 10.7 us -> 9.55 us
where the time goes in v2:
time: 112 us; the launch traced here: 111 us
  Pallas kernels  101 us (90%)
  local copies, waits for them, and re-layouts  9.55 us (9%)
    pallas_call x2, Pallas kernels, fold_call(): pl.pallas_call(functools.partial(fold_kernel, extend, tile, frame), out_s...  57.6 us
    pallas_call x2, Pallas kernels, frame_grads(): pl.pallas_call(frames_kernel, out_shape=jax.ShapeDtypeStruct(ext.shape, j...  22.8 us
    pallas_call x1, Pallas kernels, extend_call(): pl.pallas_call(extend_kernel, out_shape=[jax.ShapeDtypeStruct((4, whole,...  20.6 us
    unnamed x24, local copies, waits for them, and re-layouts  9.55 us

profile of v2, /device:TPU:9, one launch (start us, length us, event | category | flops | bytes accessed | tf_op | source)
XLA Modules:
  0.0 110.7 jit_solution(1128639672573742187)
XLA Ops:
  0.0 0.8 copy.9.pos_ref
  0.8 0.0 copy-start.4
  0.8 1.7 %copy-done.4 = f32[2,2,384,384]{3,2,1,0:T(8,128)S(1)} copy-done((f32[2,2,384,384]{3,2,1,0:T(8,128)S(1)}, f32[2,2,384,384]{3,2,1,0:T(8,128)}, u32[]{:S(2)}) %copy-start.4) | copy-done | bytes 2359320
  2.4 0.8 copy-done.9
  3.3 20.6 %shard_map.82 = (f32[4,512,512]{2,1,0:T(8,128)S(1)}, f32[2,128,128]{2,1,0:T(8,128)S(1)}) custom-call(f32[4,384,384]{2,1,0:T(8,128)S(1)} %bitcast.3, f32[128,128]{1,0:T(8,128)S(1)} %copy-done.9), custom_call_target="tpu_custom_call" | custom-call | tf_op jit(solution)/shard_map/pallas_call | solution.py:385
  23.9 0.0 copy-start
  23.9 1.1 %copy-done = bf16[2,256,768]{2,1,0:T(8,128)(2,1)S(1)} copy-done((bf16[2,256,768]{2,1,0:T(8,128)(2,1)S(1)}, bf16[2,256,768]{2,1,0:T(8,128)(2,1)}, u32[]{:S(2)}) %copy-start) | copy-done | bytes 786456
  25.0 1.1 %copy-done.2 = bf16[2,768,256]{2,1,0:T(8,128)(2,1)S(1)} copy-done((bf16[2,768,256]{2,1,0:T(8,128)(2,1)S(1)}, bf16[2,768,256]{2,1,0:T(8,128)(2,1)}, u32[]{:S(2)}) %copy-start.2) | copy-done | bytes 786456
  26.2 1.0 copy-done.5
  27.2 0.9 copy-done.7
  28.1 0.7 copy-done.10
  28.8 11.4 %shard_map.83.grad = f32[4,512,512]{2,1,0:T(8,128)S(1)} custom-call(s32[1,4]{1,0:T(1,128)S(1)} %copy-done.10, s32[8,2]{1,0:T(8,128)S(1)} %copy.9.pos_ref, f32[4,512,512]{2,1,0:T(8,128)S(1)} %get-tuple-element.7.ext, f32[2,128,128]{2,1,0:T(8,128)S(1)} %copy-done.7, f32[2,128,128]{2,1,0:T(8,128)S(1)} %get-tuple-element.8.kern_ref, ...), custom_call_target="tpu_custom_call" | custom-call | tf_op jit(solution)/shard_map/pallas_call | solution.py:148
  40.2 0.0 copy-start.1
  40.2 0.0 copy-start.3
  40.2 0.0 copy-start.6
  40.2 0.0 copy-start.8
  40.2 36.5 %shard_map.84.ext = f32[4,512,512]{2,1,0:T(8,128)S(1)} custom-call(f32[4,512,512]{2,1,0:T(8,128)S(1)} %get-tuple-element.7.ext, f32[4,512,512]{2,1,0:T(8,128)S(1)} %shard_map.83.grad), custom_call_target="tpu_custom_call" | custom-call | tf_op jit(solution)/shard_map/pallas_call | solution.py:412
  76.7 0.0 copy-done.1
  76.7 0.0 copy-done.3
  76.7 0.0 copy-done.6
  76.8 0.0 copy-done.8
  76.8 11.4 %shard_map.85.grad = f32[4,512,512]{2,1,0:T(8,128)S(1)} custom-call(s32[1,4]{1,0:T(1,128)S(1)} %copy-done.10, s32[8,2]{1,0:T(8,128)S(1)} %copy.9.pos_ref, f32[4,512,512]{2,1,0:T(8,128)S(1)} %shard_map.84.ext, f32[2,128,128]{2,1,0:T(8,128)S(1)} %copy-done.8, f32[2,128,128]{2,1,0:T(8,128)S(1)} %get-tuple-element.8.kern_ref, f32[8,128,128]{2,1,0:T(8,128)S(1)} %copy-done.6, ...), custom_call_target="tpu_custom_call" | custom-call | tf_op jit(solution)/shard_map/pallas_call | solution.py:148
  88.2 21.1 %shard_map.86 = f32[4,384,384]{2,1,0:T(8,128)S(1)} custom-call(f32[4,512,512]{2,1,0:T(8,128)S(1)} %shard_map.84.ext, f32[4,512,512]{2,1,0:T(8,128)S(1)} %shard_map.85.grad), custom_call_target="tpu_custom_call" | custom-call | tf_op jit(solution)/shard_map/pallas_call | solution.py:412
  109.3 1.4 %copy.12 = f32[2,2,384,384]{3,2,1,0:T(8,128)} copy(f32[2,2,384,384]{3,2,1,0:T(8,128)S(1)} %bitcast.2) | data formatting | bytes 4718592
  (5 shorter events, 0.0 us)
Async XLA Ops:
  0.8 1.7 %copy-start.4 = (f32[2,2,384,384]{3,2,1,0:T(8,128)S(1)}, f32[2,2,384,384]{3,2,1,0:T(8,128)}, u32[]{:S(2)}) copy-start(f32[2,2,384,384]{3,2,1,0:T(8,128)} %param.8) | copy-start | bytes 7077892
  2.4 0.8 copy-start.9
  23.9 1.1 %copy-start = (bf16[2,256,768]{2,1,0:T(8,128)(2,1)S(1)}, bf16[2,256,768]{2,1,0:T(8,128)(2,1)}, u32[]{:S(2)}) copy-start(bf16[2,256,768]{2,1,0:T(8,128)(2,1)} %constant.5.clone.ltab_ref) | copy-start | bytes 2359300
  25.0 1.1 %copy-start.2 = (bf16[2,768,256]{2,1,0:T(8,128)(2,1)S(1)}, bf16[2,768,256]{2,1,0:T(8,128)(2,1)}, u32[]{:S(2)}) copy-start(bf16[2,768,256]{2,1,0:T(8,128)(2,1)} %constant.4.clone.rtab_ref) | copy-start | bytes 2359300
  26.2 1.0 copy-start.5
  27.2 0.9 copy-start.7
  28.1 0.7 copy-start.10
  40.2 36.5 %copy-start.1 = (bf16[2,256,768]{2,1,0:T(8,128)(2,1)S(1)}, bf16[2,256,768]{2,1,0:T(8,128)(2,1)}, u32[]{:S(2)}) copy-start(bf16[2,256,768]{2,1,0:T(8,128)(2,1)} %constant.5.clone.ltab_ref) | copy-start | bytes 2359300
  40.2 36.5 %copy-start.3 = (bf16[2,768,256]{2,1,0:T(8,128)(2,1)S(1)}, bf16[2,768,256]{2,1,0:T(8,128)(2,1)}, u32[]{:S(2)}) copy-start(bf16[2,768,256]{2,1,0:T(8,128)(2,1)} %constant.4.clone.rtab_ref) | copy-start | bytes 2359300
  40.2 36.5 %copy-start.6 = (f32[8,128,128]{2,1,0:T(8,128)S(1)}, f32[8,128,128]{2,1,0:T(8,128)}, u32[]{:S(2)}) copy-start(f32[8,128,128]{2,1,0:T(8,128)} %meas_ref.3) | copy-start | bytes 1572868
  40.2 36.5 %copy-start.8 = (f32[2,128,128]{2,1,0:T(8,128)S(1)}, f32[2,128,128]{2,1,0:T(8,128)}, u32[]{:S(2)}) copy-start(f32[2,128,128]{2,1,0:T(8,128)} %probe_ref.3) | copy-start | bytes 393220

commit v3 on v2

--- a/solution.py
+++ b/solution.py
@@ -9,7 +9,8 @@
 from jax.sharding import PartitionSpec as P
 
 ITERS = 2
-GROUP = 4
+GROUP = 8
+CHAIN = 2
 SUB = 8
 
 step_size = 0.2
@@ -36,6 +37,17 @@
     return high, low
 
 
+def in_chains(transform):
+    def over_all(waves, table):
+        out = []
+        for i in range(0, len(waves), CHAIN):
+            out += transform(waves[i : i + CHAIN], table)
+        return out
+
+    return over_all
+
+
+@in_chains
 def by_right(waves, table):
     size = waves[0][0].shape[0]
     x = jnp.concatenate([jnp.concatenate(wave, axis=1) for wave in waves], axis=0)
@@ -49,6 +61,7 @@
     ]
 
 
+@in_chains
 def by_left(waves, table):
     size = waves[0][0].shape[0]
     x = jnp.concatenate([jnp.concatenate(wave, axis=0) for wave in waves], axis=1)
@@ -217,7 +230,9 @@
             pl.when(has_target)(copy.wait_send)
 
 
-def extend_kernel(main, phase, ext, kern, send_sems, recv_sems, sem):
+def extend_kernel(held, main, phase_hbm, *rest):
+    later, (ext, kern), near = rest[:held], rest[held : held + 2], rest[held + 2 : 2 * held + 2]
+    phase, send_sems, recv_sems, sems = rest[2 * held + 2 :]
     tile = main.shape[2]
     frame = phase.shape[0]
     chunks = tile // frame
@@ -241,14 +256,21 @@
     around.meet()
     for number in range(chunks + 1):
         sends.start(number)
-    load = pltpu.make_async_copy(main, ext.at[:, core, core], sem)
-    load.start()
+    phase_load = pltpu.make_async_copy(phase_hbm, phase, sems.at[0])
+    loads = [pltpu.make_async_copy(main, ext.at[:, core, core], sems.at[1])] + [
+        pltpu.make_async_copy(src, dst, sems.at[2 + i]) for i, (src, dst) in enumerate(zip(later, near))
+    ]
+    phase_load.start()
+    for load in loads:
+        load.start()
+    phase_load.wait()
     kern[0] = jnp.cos(phase[...])
     kern[1] = jnp.sin(phase[...])
     clear_edges(around, ext, tile, frame)
     sends.arrived(0)
     sends.start(chunks + 1)
-    load.wait()
+    for load in loads:
+        load.wait()
     for number in range(1, chunks + 2):
         sends.arrived(number)
     sends.drain()
@@ -376,29 +398,31 @@
     sends.drain()
 
 
-def extend_call(main, phase):
+def extend_call(main, phase, later):
     tile, frame = main.shape[2], phase.shape[0]
-    anywhere = pl.BlockSpec(memory_space=pl.ANY)
+    outside = pl.BlockSpec(memory_space=pltpu.HBM)
     vmem = pl.BlockSpec(memory_space=pltpu.VMEM)
     copies = tile // frame + 2
     whole = tile + frame
     return pl.pallas_call(
-        extend_kernel,
+        functools.partial(extend_kernel, len(later)),
         out_shape=[
             jax.ShapeDtypeStruct((4, whole, whole), jnp.float32),
             jax.ShapeDtypeStruct((2, frame, frame), jnp.float32),
-        ],
-        in_specs=[anywhere, vmem],
-        out_specs=[vmem] * 2,
+        ]
+        + [jax.ShapeDtypeStruct(x.shape, x.dtype) for x in later],
+        in_specs=[outside] * (2 + len(later)),
+        out_specs=[vmem] * (2 + len(later)),
         scratch_shapes=[
+            pltpu.VMEM(phase.shape, jnp.float32),
             pltpu.SemaphoreType.DMA((copies,)),
             pltpu.SemaphoreType.DMA((copies,)),
-            pltpu.SemaphoreType.DMA,
+            pltpu.SemaphoreType.DMA((2 + len(later),)),
         ],
         compiler_params=pltpu.CompilerParams(
             collective_id=0, has_side_effects=True, vmem_limit_bytes=16 << 20
         ),
-    )(main, phase)
+    )(*[pltpu.with_memory_space_constraint(x, pltpu.HBM) for x in (main, phase, *later)])
 
 
 def fold_call(ext, grad, frame, extend):
@@ -433,9 +457,11 @@
     tile = object_tiles.shape[3]
     frame = probe_field.shape[1]
     tables = [jnp.asarray(t) for t in dft_tables(frame)]
-    ext, kern = extend_call(object_tiles.reshape(4, tile, tile), prop_phase)
+    later = (counts, positions, probe_field, intensity, *tables)
+    ext, kern, *near = extend_call(object_tiles.reshape(4, tile, tile), prop_phase, later)
+    counts, positions, probe, measured, *tables = near
     for iteration in range(ITERS):
-        grad = frame_grads(counts, positions, ext, probe_field, kern, intensity, tables)
+        grad = frame_grads(counts, positions, ext, probe, kern, measured, tables)
         ext = fold_call(ext, grad, frame, iteration < ITERS - 1)
     return ext.reshape(object_tiles.shape)
 

time: 112 us -> 99.2 us (0.89)
  local copies, waits for them, and re-layouts: 9.55 us -> 2.75 us
  Pallas kernels: 101 us -> 95.9 us
    unnamed x24 -> x2, local copies, waits for them, and re-layouts: 9.55 us -> 2.75 us
    pallas_call x2, Pallas kernels: 22.8 us -> 16.2 us  [frame_grads(): pl.pallas_call(frames_kernel, out_shape=jax.ShapeDtypeStruct(ext.shape, j...]
    pallas_call x2, Pallas kernels: 57.6 us -> 58.8 us  [fold_call(): pl.pallas_call(functools.partial(fold_kernel, extend, tile, frame), out_s...]
where the time goes in v3:
time: 99.2 us; the launch traced here: 98.7 us
  Pallas kernels  95.9 us (97%)
  local copies, waits for them, and re-layouts  2.75 us (3%)
    pallas_call x2, Pallas kernels, fold_call(): pl.pallas_call(functools.partial(fold_kernel, extend, tile, frame), out_s...  58.8 us
    pallas_call x1, Pallas kernels, extend_call(): pl.pallas_call(functools.partial(extend_kernel, len(later)), out_shape=[j...  20.9 us
    pallas_call x2, Pallas kernels, frame_grads(): pl.pallas_call(frames_kernel, out_shape=jax.ShapeDtypeStruct(ext.shape, j...  16.2 us
    unnamed x2, local copies, waits for them, and re-layouts  2.75 us

profile of v3, /device:TPU:9, one launch (start us, length us, event | category | flops | bytes accessed | tf_op | source)
XLA Modules:
  0.0 98.7 jit_solution(8466399839431040287)
XLA Ops:
  0.0 1.3 %copy.9.rest_1_ = s32[8,2]{1,0:T(8,128)} copy(s32[8,2]{0,1:T(2,128)} %param.12) | data formatting | bytes 128 | tf_op args[4]
  1.3 20.9 %shard_map.82 = (f32[4,512,512]{2,1,0:T(8,128)S(1)}, f32[2,128,128]{2,1,0:T(8,128)S(1)}, s32[1,4]{1,0:T(1,128)S(1)}, s32[8,2]{1,0:T(8,128)S(1)}, f32[2,128,128]{...) custom-call(f32[4,384,384]{2,1,0:T(8,128)} %bitcast.3, ...), custom_call_target="tpu_custom_call" | custom-call | tf_op jit(solution)/shard_map/pallas_call | solution.py:407
  22.2 8.0 %shard_map.83.grad = f32[4,512,512]{2,1,0:T(8,128)S(1)} custom-call(s32[1,4]{1,0:T(1,128)S(1)} %get-tuple-element.14.counts_ref, s32[8,2]{1,0:T(8,128)S(1)} %get-tuple-element.15.pos_ref, f32[4,512,512]{2,1,0:T(8,128)S(1)} %get-tuple-element.13.ext, f32[2,128,128]{2,1,0:T(8,128)S(1)} %get-tuple-element.16.probe_ref, ...), custom_call_target="tpu_custom_call" | custom-call | tf_op jit(solution)/shard_map/pallas_call | solution.py:161
  30.3 37.9 %shard_map.84.ext = f32[4,512,512]{2,1,0:T(8,128)S(1)} custom-call(f32[4,512,512]{2,1,0:T(8,128)S(1)} %get-tuple-element.13.ext, f32[4,512,512]{2,1,0:T(8,128)S(1)} %shard_map.83.grad), custom_call_target="tpu_custom_call" | custom-call | tf_op jit(solution)/shard_map/pallas_call | solution.py:436
  68.2 8.2 %shard_map.85.grad = f32[4,512,512]{2,1,0:T(8,128)S(1)} custom-call(s32[1,4]{1,0:T(1,128)S(1)} %get-tuple-element.14.counts_ref, s32[8,2]{1,0:T(8,128)S(1)} %get-tuple-element.15.pos_ref, f32[4,512,512]{2,1,0:T(8,128)S(1)} %shard_map.84.ext, f32[2,128,128]{2,1,0:T(8,128)S(1)} %get-tuple-element.16.probe_ref, f32[2,128,128]{2,1,0:T(8,128)S(1)} %get-tuple-element.17.kern_ref, ...), custom_call_target="tpu_custom_call" | custom-call | tf_op jit(solution)/shard_map/pallas_call | solution.py:161
  76.4 20.9 %shard_map.86 = f32[4,384,384]{2,1,0:T(8,128)S(1)} custom-call(f32[4,512,512]{2,1,0:T(8,128)S(1)} %shard_map.84.ext, f32[4,512,512]{2,1,0:T(8,128)S(1)} %shard_map.85.grad), custom_call_target="tpu_custom_call" | custom-call | tf_op jit(solution)/shard_map/pallas_call | solution.py:436
  97.3 1.4 %copy.11 = f32[2,2,384,384]{3,2,1,0:T(8,128)} copy(f32[2,2,384,384]{3,2,1,0:T(8,128)S(1)} %bitcast.2) | data formatting | bytes 4718592

commit v4 on v3

--- a/solution.py
+++ b/solution.py
@@ -101,8 +101,8 @@
             slot = group * GROUP + i
             here = jnp.minimum(slot, slots - 1)
             weight = (slot < count).astype(jnp.float32)
-            top = pos_ref[here, 0]
-            left = pos_ref[here, 1]
+            top = pos_ref[0, here]
+            left = pos_ref[1, here]
             block = left // frame
             shift = left - block * frame
             near = pl.ds(pl.multiple_of(block * frame, frame), frame)
@@ -457,7 +457,7 @@
     tile = object_tiles.shape[3]
     frame = probe_field.shape[1]
     tables = [jnp.asarray(t) for t in dft_tables(frame)]
-    later = (counts, positions, probe_field, intensity, *tables)
+    later = (counts, positions.T, probe_field, intensity, *tables)
     ext, kern, *near = extend_call(object_tiles.reshape(4, tile, tile), prop_phase, later)
     counts, positions, probe, measured, *tables = near
     for iteration in range(ITERS):

time: 99.2 us -> 97.8 us (0.986)
  local copies, waits for them, and re-layouts: 2.75 us -> 1.41 us
    unnamed x2 -> x1, local copies, waits for them, and re-layouts: 2.75 us -> 1.41 us
where the time goes in v4:
time: 97.8 us; the launch traced here: 97.3 us
  Pallas kernels  95.8 us (98%)
  local copies, waits for them, and re-layouts  1.41 us (1%)
    pallas_call x2, Pallas kernels, fold_call(): pl.pallas_call(functools.partial(fold_kernel, extend, tile, frame), out_s...  58.8 us
    pallas_call x1, Pallas kernels, extend_call(): pl.pallas_call(functools.partial(extend_kernel, len(later)), out_shape=[j...  20.9 us
    pallas_call x2, Pallas kernels, frame_grads(): pl.pallas_call(frames_kernel, out_shape=jax.ShapeDtypeStruct(ext.shape, j...  16.2 us

profile of v4, /device:TPU:9, one launch (start us, length us, event | category | flops | bytes accessed | tf_op | source)
XLA Modules:
  0.0 97.3 jit_solution(5357017187348751771)
XLA Ops:
  0.0 20.9 %shard_map.82 = (f32[4,512,512]{2,1,0:T(8,128)S(1)}, f32[2,128,128]{2,1,0:T(8,128)S(1)}, s32[1,4]{1,0:T(1,128)S(1)}, s32[2,8]{1,0:T(2,128)S(1)}, f32[2,128,128]{...) custom-call(f32[4,384,384]{2,1,0:T(8,128)} %bitcast.4, ...), custom_call_target="tpu_custom_call" | custom-call | tf_op jit(solution)/shard_map/pallas_call | solution.py:407
  20.9 8.0 %shard_map.83.grad = f32[4,512,512]{2,1,0:T(8,128)S(1)} custom-call(s32[1,4]{1,0:T(1,128)S(1)} %get-tuple-element.14.counts_ref, s32[2,8]{1,0:T(2,128)S(1)} %get-tuple-element.15.pos_ref, f32[4,512,512]{2,1,0:T(8,128)S(1)} %get-tuple-element.13.ext, f32[2,128,128]{2,1,0:T(8,128)S(1)} %get-tuple-element.16.probe_ref, ...), custom_call_target="tpu_custom_call" | custom-call | tf_op jit(solution)/shard_map/pallas_call | solution.py:161
  28.9 37.9 %shard_map.84.ext = f32[4,512,512]{2,1,0:T(8,128)S(1)} custom-call(f32[4,512,512]{2,1,0:T(8,128)S(1)} %get-tuple-element.13.ext, f32[4,512,512]{2,1,0:T(8,128)S(1)} %shard_map.83.grad), custom_call_target="tpu_custom_call" | custom-call | tf_op jit(solution)/shard_map/pallas_call | solution.py:436
  66.8 8.2 %shard_map.85.grad = f32[4,512,512]{2,1,0:T(8,128)S(1)} custom-call(s32[1,4]{1,0:T(1,128)S(1)} %get-tuple-element.14.counts_ref, s32[2,8]{1,0:T(2,128)S(1)} %get-tuple-element.15.pos_ref, f32[4,512,512]{2,1,0:T(8,128)S(1)} %shard_map.84.ext, f32[2,128,128]{2,1,0:T(8,128)S(1)} %get-tuple-element.16.probe_ref, f32[2,128,128]{2,1,0:T(8,128)S(1)} %get-tuple-element.17.kern_ref, ...), custom_call_target="tpu_custom_call" | custom-call | tf_op jit(solution)/shard_map/pallas_call | solution.py:161
  75.0 20.9 %shard_map.86 = f32[4,384,384]{2,1,0:T(8,128)S(1)} custom-call(f32[4,512,512]{2,1,0:T(8,128)S(1)} %shard_map.84.ext, f32[4,512,512]{2,1,0:T(8,128)S(1)} %shard_map.85.grad), custom_call_target="tpu_custom_call" | custom-call | tf_op jit(solution)/shard_map/pallas_call | solution.py:436
  95.9 1.4 %copy.10 = f32[2,2,384,384]{3,2,1,0:T(8,128)} copy(f32[2,2,384,384]{3,2,1,0:T(8,128)S(1)} %bitcast.3) | data formatting | bytes 4718592
